TPU v7x, 768 devices: a whole 4x8x12 slice. The times are simulated.
768 devices in a mesh: seq: 4 (over z_hi), expert: 48 (over y, z_lo, core), rep: 4 (over x).
Axes of the slice: x: 4, y: 8, z: 12 (z_hi: 4, z_lo: 3; z = z_hi * 3 + z_lo), core: 2. Of those that a mesh axis runs over, the one named last changes fastest.
Arguments:
- query_rows: bfloat16 [48, 2048, 512], P('expert', ('seq', 'rep')), may hold values from -150 to 150
- key_rows: bfloat16 [48, 2048, 512], P('expert', ('seq', 'rep')), may hold values from -150 to 150
- value_rows: bfloat16 [48, 2048, 512], P('expert', ('seq', 'rep')), may hold values from -6 to 6
- doc_lengths: int32 [48, 8], P('expert'), may hold values from 1 to 1024, 2048 in all within a row
- residual: bfloat16 [48, 2048, 512], P('expert', ('seq', 'rep')), may hold values from -6 to 6
- out_proj: bfloat16 [512, 512], replicated, may hold values from -0.25 to 0.25
- router: bfloat16 [512, 48], replicated, may hold values from -0.5 to 0.5
- expert_choice: int32 [48, 2048, 1], P('expert', ('seq', 'rep')), may hold values from 0 to 47, as said below
- weight_in: bfloat16 [48, 512, 512], P('expert'), may hold values from -0.25 to 0.25
- weight_out: bfloat16 [48, 512, 512], P('expert'), may hold values from -0.5 to 0.5
- grad_out: bfloat16 [48, 2048, 512], P('expert', ('seq', 'rep')), may hold values from -6 to 6
Outputs:
- layer_out: bfloat16 [48, 2048, 512], P('expert', ('seq', 'rep'))
- grad_mixed: bfloat16 [48, 2048, 512], P('expert', ('seq', 'rep'))
- grad_weight_in: float32 [48, 512, 512], P('expert', ('seq', 'rep'))
- grad_weight_out: float32 [48, 512, 512], P('expert', ('seq', 'rep'))
Inputs may be any that keep to these rules, and one draw needn't show every extreme that they name: `expert_choice`: A routing group is one index of seq and one of rep; each group has one hot expert, the same on all of the group's devices. Among one device's tokens, its group's hot expert is named between 5 and 16 times, exactly 16 times on some device and 4 + 1 times on some device; every other expert is named at most 4 times, and on every device some expert other than the hot one is named exactly 4 times. `doc_lengths`: each sequence's lengths sum to 2048; the longest is exactly half of 2048.
All inputs are finite; a program needn't handle non-finite values.
Results may differ from a plain program's by a relative error of at most 0.02.
Values may be sent and summed in bfloat16 or wider, within the bound.
A program may use at most 32 MiB of HBM per device.

v0:
```python
import math

import jax
import jax.numpy as jnp
from jax import lax
from jax.sharding import PartitionSpec as P

D = 512
H = 16
HD = 32


norm_eps = 1e-06
masked_score = -1e30


def spread(x, axis, root):
    mine = lax.axis_index(axis) == root
    return lax.psum(jnp.where(mine, x, jnp.zeros_like(x)), axis)


def document_ids(lengths, positions):
    boundaries = jnp.cumsum(lengths)
    return jnp.sum((positions[:, None] >= boundaries[None, :-1]).astype(jnp.int32), axis=1)


def expert_pass(token_rows, grad_rows, weight_up, weight_down):
    hidden_pre = jnp.dot(token_rows, weight_up, preferred_element_type=jnp.float32)
    sigmoid_pre = jax.nn.sigmoid(hidden_pre)
    activated = (hidden_pre * sigmoid_pre).astype(jnp.bfloat16)
    produced = jnp.dot(activated, weight_down, preferred_element_type=jnp.float32).astype(
        jnp.bfloat16
    )
    act_grad = jnp.dot(grad_rows, weight_down.T, preferred_element_type=jnp.float32)
    pre_grad = (act_grad * sigmoid_pre * (1.0 + hidden_pre * (1.0 - sigmoid_pre))).astype(
        jnp.bfloat16
    )
    token_grad = jnp.dot(pre_grad, weight_up.T, preferred_element_type=jnp.float32).astype(
        jnp.bfloat16
    )
    up_grad = jnp.dot(token_rows.T, pre_grad, preferred_element_type=jnp.float32)
    down_grad = jnp.dot(activated.T, grad_rows, preferred_element_type=jnp.float32)
    return (produced, token_grad, up_grad, down_grad)


def empty_state(head_count, row_count):
    return (
        jnp.full((head_count, row_count), masked_score, jnp.float32),
        jnp.zeros((head_count, row_count), jnp.float32),
        jnp.zeros((head_count, row_count, HD), jnp.float32),
    )


def attend_fold(
    fold_state, query_heads, query_pos, query_docs, key_heads, value_heads, key_pos, key_docs
):
    maxima, totals, accum = fold_state
    scores = jnp.einsum(
        "qhd,khd->hqk", query_heads, key_heads, preferred_element_type=jnp.float32
    ) * (1.0 / math.sqrt(HD))
    visible = (key_pos[None, :] <= query_pos[:, None]) & (key_docs[None, :] == query_docs[:, None])
    scores = jnp.where(visible[None], scores, masked_score)
    new_max = jnp.maximum(maxima, jnp.max(scores, axis=2))
    weights = jnp.where(visible[None], jnp.exp(scores - new_max[:, :, None]), 0.0)
    factor = jnp.exp(maxima - new_max)
    totals = totals * factor + jnp.sum(weights, axis=2)
    accum = accum * factor[:, :, None] + jnp.einsum(
        "hqk,khd->hqd",
        weights.astype(jnp.bfloat16),
        value_heads,
        preferred_element_type=jnp.float32,
    )
    return (new_max, totals, accum)


def finish_heads(fold_state):
    maxima, totals, accum = fold_state
    result = accum / totals[:, :, None]
    return result.transpose(1, 0, 2).reshape(result.shape[1], -1).astype(jnp.bfloat16)


def local(
    query_rows,
    key_rows,
    value_rows,
    doc_lengths,
    residual,
    out_proj,
    router,
    expert_choice,
    weight_in,
    weight_out,
    grad_out,
):
    tok_count = query_rows.shape[1]
    seq_rank = lax.axis_index(("seq", "rep"))
    lengths = doc_lengths[0]
    query_pos = seq_rank * tok_count + jnp.arange(tok_count, dtype=jnp.int32)
    query_heads = query_rows[0].reshape(tok_count, H, HD)
    query_docs = document_ids(lengths, query_pos)
    key_part = lax.all_gather(key_rows, ("seq", "rep"), axis=1, tiled=True)
    value_part = lax.all_gather(value_rows, ("seq", "rep"), axis=1, tiled=True)
    span = key_part.shape[1]
    block = math.gcd(span, 512)

    def key_block(state, block_index):
        first_row = block_index * block
        key_block_rows = lax.dynamic_slice_in_dim(key_part[0], first_row, block, 0).reshape(
            block, H, HD
        )
        value_block_rows = lax.dynamic_slice_in_dim(value_part[0], first_row, block, 0).reshape(
            block, H, HD
        )
        key_pos = first_row + jnp.arange(block, dtype=jnp.int32)
        return (
            attend_fold(
                state,
                query_heads,
                query_pos,
                query_docs,
                key_block_rows,
                value_block_rows,
                key_pos,
                document_ids(lengths, key_pos),
            ),
            None,
        )

    result_state, unused = lax.scan(
        key_block, empty_state(H, tok_count), jnp.arange(span // block, dtype=jnp.int32)
    )
    attended = finish_heads(result_state)
    mixed = (
        residual[0].astype(jnp.float32)
        + jnp.dot(attended, out_proj, preferred_element_type=jnp.float32)
    ).astype(jnp.bfloat16)
    mixed_f = mixed.astype(jnp.float32)
    inv_rms = lax.rsqrt(jnp.mean(mixed_f * mixed_f, axis=1, keepdims=True) + norm_eps)
    normed = (mixed_f * inv_rms).astype(jnp.bfloat16)
    expert_count = router.shape[1]
    chosen = expert_choice[0, :, 0]
    expert_ids = jnp.arange(expert_count, dtype=jnp.int32)
    one_hot = chosen[:, None] == expert_ids[None, :]
    logits = jnp.dot(normed, router, preferred_element_type=jnp.float32)
    gate_value = jax.nn.sigmoid(jnp.sum(jnp.where(one_hot, logits, 0.0), axis=1))
    grad_rows = grad_out[0]
    scaled_grad = (gate_value[:, None] * grad_rows.astype(jnp.float32)).astype(jnp.bfloat16)
    capacity = max(2, (3 * tok_count + 2 * expert_count - 1) // (2 * expert_count))
    hot_capacity = min(4 * capacity, tok_count // 2)
    route_counts = jnp.sum(one_hot.astype(jnp.int32), axis=0)
    hot_id = jnp.sum(jnp.where(route_counts > capacity, expert_ids, 0))
    is_hot = chosen == hot_id
    cold_token = jnp.logical_not(is_hot)
    cold_hits = (one_hot & cold_token[:, None]).astype(jnp.int32)
    slot_rank = jnp.sum(jnp.cumsum(cold_hits, axis=0) * cold_hits, axis=1) - 1
    slots = jnp.where(cold_token, chosen * capacity + slot_rank, expert_count * capacity)
    send_rows = (
        jnp.zeros((expert_count * capacity, D), jnp.bfloat16)
        .at[slots]
        .set(normed, mode="drop")
        .reshape(expert_count, capacity, D)
    )
    send_grads = (
        jnp.zeros((expert_count * capacity, D), jnp.bfloat16)
        .at[slots]
        .set(scaled_grad, mode="drop")
        .reshape(expert_count, capacity, D)
    )
    got_rows, got_grads = (
        lax.all_to_all(send_rows, "expert", split_axis=0, concat_axis=0, tiled=True),
        lax.all_to_all(send_grads, "expert", split_axis=0, concat_axis=0, tiled=True),
    )
    produced, token_grads, grad_in_own, grad_out_own = expert_pass(
        got_rows.reshape(-1, D), got_grads.reshape(-1, D), weight_in[0], weight_out[0]
    )
    back_out, back_grad = (
        lax.all_to_all(
            produced.reshape(expert_count, capacity, D),
            "expert",
            split_axis=0,
            concat_axis=0,
            tiled=True,
        ),
        lax.all_to_all(
            token_grads.reshape(expert_count, capacity, D),
            "expert",
            split_axis=0,
            concat_axis=0,
            tiled=True,
        ),
    )
    safe_slots = jnp.clip(slots, 0, expert_count * capacity - 1)
    expert_result = back_out.reshape(-1, D)[safe_slots]
    normed_grad = back_grad.reshape(-1, D)[safe_slots]
    hot_in, hot_out = (
        spread(weight_in[0], "expert", hot_id),
        spread(weight_out[0], "expert", hot_id),
    )
    hot_rank = jnp.cumsum(is_hot.astype(jnp.int32)) - 1
    hot_slot = jnp.where(is_hot, hot_rank, hot_capacity)
    hot_rows = jnp.zeros((hot_capacity, D), jnp.bfloat16).at[hot_slot].set(normed, mode="drop")
    hot_grad_rows = (
        jnp.zeros((hot_capacity, D), jnp.bfloat16).at[hot_slot].set(scaled_grad, mode="drop")
    )
    hot_result, hot_grad, hot_grad_in, hot_grad_out = expert_pass(
        hot_rows, hot_grad_rows, hot_in, hot_out
    )
    summed_in, summed_out = lax.psum((hot_grad_in, hot_grad_out), "expert")
    owner_here = hot_id == lax.axis_index("expert")
    grad_in_own = grad_in_own + jnp.where(owner_here, summed_in, 0.0)
    grad_out_own = grad_out_own + jnp.where(owner_here, summed_out, 0.0)
    safe_hot = jnp.clip(hot_slot, 0, hot_capacity - 1)
    expert_result = jnp.where(is_hot[:, None], hot_result[safe_hot], expert_result)
    normed_grad = jnp.where(is_hot[:, None], hot_grad[safe_hot], normed_grad)
    result_f = expert_result.astype(jnp.float32)
    layer_out = (mixed_f + gate_value[:, None] * result_f).astype(jnp.bfloat16)
    gate_grad = jnp.sum(grad_rows.astype(jnp.float32) * result_f, axis=1)
    logit_grad = gate_grad * gate_value * (1.0 - gate_value)
    router_cols = jnp.dot(
        one_hot.astype(jnp.bfloat16), router.T, preferred_element_type=jnp.float32
    )
    total_grad = normed_grad.astype(jnp.float32) + logit_grad[:, None] * router_cols
    mean_term = jnp.mean(total_grad * mixed_f, axis=1, keepdims=True)
    input_grad = inv_rms * total_grad - mixed_f * inv_rms * inv_rms * inv_rms * mean_term
    grad_mixed = (grad_rows.astype(jnp.float32) + input_grad).astype(jnp.bfloat16)
    share_in, share_out = (
        lax.psum_scatter(
            grad_in_own.astype(jnp.bfloat16), ("seq", "rep"), scatter_dimension=0, tiled=True
        ).astype(jnp.float32),
        lax.psum_scatter(
            grad_out_own.astype(jnp.bfloat16), ("seq", "rep"), scatter_dimension=0, tiled=True
        ).astype(jnp.float32),
    )
    return (layer_out[None], grad_mixed[None], share_in[None], share_out[None])


def solution(mesh):
    in_specs = (
        P("expert", ("seq", "rep"), None),
        P("expert", ("seq", "rep"), None),
        P("expert", ("seq", "rep"), None),
        P("expert", None),
        P("expert", ("seq", "rep"), None),
        P(),
        P(),
        P("expert", ("seq", "rep"), None),
        P("expert", None, None),
        P("expert", None, None),
        P("expert", ("seq", "rep"), None),
    )
    out_specs = (
        P("expert", ("seq", "rep"), None),
        P("expert", ("seq", "rep"), None),
        P("expert", ("seq", "rep"), None),
        P("expert", ("seq", "rep"), None),
    )
    return jax.shard_map(local, mesh=mesh, in_specs=in_specs, out_specs=out_specs, check_vma=False)
```

profile of v0, /device:TPU:1, one launch (start us, length us, event | category | flops | bytes accessed | tf_op | source)
XLA Modules:
  0.0 1348.6 jit_solution(9980705147949630081)
XLA Ops:
  8.1 1.7 copy.38
  9.8 1.7 copy.40
  11.6 0.8 reduce-window.13
  12.4 1.0 copy.39
  13.4 0.8 convert_reduce_fusion.1
  14.2 0.6 fusion.54
  15.4 1.2 fusion.56
  16.8 0.7 multiply_bitcast_fusion
  17.5 1.2 fusion.57
  18.8 0.7 fusion.49
  19.8 0.7 select_reduce_fusion
  21.1 88.4 %all-gather.3.cloned.1.call-done = bf16[1,2048,512]{1,2,0:T(8,128)(2,1)} async-done(((bf16[1,128,512]{1,2,0:T(8,128)(2,1)}), bf16[1,2048,512]{1,2,0:T(8,128)(2,1)}) %all-gather.3.cloned.1.call-update) | async-done | bytes 2097168 | tf_op jit(solution)/shard_map/all_gather | solution.py:101
  109.5 89.1 %all-gather.5.cloned.1.call-done = bf16[1,2048,512]{1,2,0:T(8,128)(2,1)} async-done(((bf16[1,128,512]{1,2,0:T(8,128)(2,1)}), bf16[1,2048,512]{1,2,0:T(8,128)(2,1)}) %all-gather.5.cloned.1.call-update) | async-done | bytes 2097168 | tf_op jit(solution)/shard_map/all_gather | solution.py:102
  198.6 42.3 %while.17 = (s32[]{:T(128)}, f32[16,128]{1,0:T(8,128)S(1)}, f32[16,128]{1,0:T(8,128)S(1)}, f32[16,128,32]{1,2,0:T(8,128)S(1)}, s32[4]{0:T(128)S(1)}, /*index=5*/...) while((s32[]{:T(128)}, f32[16,128]{1,0:T(8,128)S(1)}, ...), condition=%wide.region_6.7_spmd.clone, body=%wide.region_2.6_spmd.clone.sunk | while | flops 148263552 | bytes 33566548 | solution.py:129
  200.2 1.3 constant_dynamic-slice_fusion.3
  201.5 2.9 fusion.96
  204.4 3.3 fusion.97
  207.9 1.3 fusion.99
  210.8 1.3 constant_dynamic-slice_fusion.3
  212.1 2.9 fusion.96
  215.0 3.3 fusion.97
  218.5 1.3 fusion.99
  221.4 1.3 constant_dynamic-slice_fusion.3
  222.7 2.9 fusion.96
  225.6 3.3 fusion.97
  229.0 1.3 fusion.99
  232.0 1.3 constant_dynamic-slice_fusion.3
  233.3 2.9 fusion.96
  236.2 3.3 fusion.97
  239.6 1.3 fusion.99
  241.4 1.2 scatter_custom_fusion.1
  242.6 0.7 reshape.291
  243.3 8.1 all-to-all-start
  251.4 1.1 bitcast_select_fusion.1
  252.5 1.1 scatter_custom_fusion
  253.6 7.4 all-to-all-done
  261.6 0.7 reshape.293
  262.4 5.5 all-to-all-start.1
  267.9 389.6 %all-reduce.7.cloned.1.call-done = (bf16[512,512]{1,0:T(8,128)(2,1)}, bf16[512,512]{1,0:T(8,128)(2,1)}) async-done(((bf16[512,512]{1,0:T(8,128)(2,1)}, bf16[512,512]{1,0:T(8,128)(2,1)}), (bf16[512,512]{1,0:T(8,128)(2,1)}, bf16[512,512]{1,0:T(8,128)(2,1)})) %all-reduce.7.cloned.1.call-update) | async-done | bytes 1048592 | tf_op jit(solution)/shard_map/psum | solution.py:19
  657.5 1.3 fusion.58
  658.7 1.2 convolution_convert_fusion.3
  660.0 0.9 gather_fusion
  661.2 0.8 gather_fusion.1
  662.2 1.1 scatter_custom_fusion.2
  663.6 1.3 fusion.55
  664.9 1.3 fusion.59
  666.3 1.2 scatter_custom_fusion.3
  667.4 0.7 reshape.295
  668.2 8.7 all-to-all-start.2
  677.7 8.8 all-to-all-done.2
  686.6 1.3 fusion.18
  687.9 412.2 %all-reduce.5.cloned.1.call-done = (f32[512,512]{1,0:T(8,128)}, f32[512,512]{1,0:T(8,128)}) async-done(((f32[512,512]{1,0:T(8,128)}, f32[512,512]{1,0:T(8,128)}), (f32[512,512]{1,0:T(8,128)}, f32[512,512]{1,0:T(8,128)})) %all-reduce.5.cloned.1.call-update) | async-done | bytes 2097168 | tf_op jit(solution)/shard_map/psum | solution.py:208
  1100.1 1.1 fusion.15
  1101.6 0.7 reshape.297
  1102.3 8.3 all-to-all-start.3
  1110.6 2.2 fusion.16
  1113.1 0.9 gather_fusion.2
  1114.0 6.3 all-to-all-done.3
  1120.3 0.8 gather_fusion.3
  1121.5 0.9 fusion.35
  1122.4 110.6 %reduce-scatter.3.cloned.1.call-done = bf16[32,512]{1,0:T(8,128)(2,1)} async-done(((bf16[512,512]{1,0:T(8,128)(2,1)}), bf16[32,512]{1,0:T(8,128)(2,1)}) %reduce-scatter.3.cloned.1.call-update) | async-done | bytes 32784 | tf_op jit(solution)/shard_map/reduce_scatter | solution.py:227
  1232.9 1.4 bitcast_convert_fusion.1
  1234.3 105.8 %reduce-scatter.5.cloned.1.call-done = bf16[32,512]{1,0:T(8,128)(2,1)} async-done(((bf16[512,512]{1,0:T(8,128)(2,1)}), bf16[32,512]{1,0:T(8,128)(2,1)}) %reduce-scatter.5.cloned.1.call-update) | async-done | bytes 32784 | tf_op jit(solution)/shard_map/reduce_scatter | solution.py:230
  1340.1 1.4 bitcast_convert_fusion
  (112 shorter events, 8.5 us)
Async XLA Ops:
  8.0 233.0 %copy-start = (bf16[512,512]{1,0:T(8,128)(2,1)S(1)}, bf16[512,512]{1,0:T(8,128)(2,1)}, u32[]{:S(2)}) copy-start(bf16[512,512]{1,0:T(8,128)(2,1)} %param.18) | copy-start | bytes 1572868
  8.0 101.5 %all-gather.3.cloned.1.call-start = ((), (), s32[]{:S(2)}) async-start(), calls=%async_computation.6 | async-start | bytes 2228224 | tf_op jit(solution)/shard_map/all_gather | solution.py:101
  9.8 188.8 %all-gather.5.cloned.1.call-start = ((), (), s32[]{:S(2)}) async-start(), calls=%async_computation.7 | async-start | bytes 2228224 | tf_op jit(solution)/shard_map/all_gather | solution.py:102
  198.6 42.4 %copy-start.9 = (bf16[1,128,512]{2,1,0:T(8,128)(2,1)S(1)}, bf16[1,128,512]{2,1,0:T(8,128)(2,1)}, u32[]{:S(2)}) copy-start(bf16[1,128,512]{2,1,0:T(8,128)(2,1)} %param.17) | copy-start | bytes 393220
  198.6 52.8 %copy-start.2 = (bf16[1,512,512]{2,1,0:T(8,128)(2,1)S(1)}, bf16[1,512,512]{2,1,0:T(8,128)(2,1)}, u32[]{:S(2)}) copy-start(bf16[1,512,512]{2,1,0:T(8,128)(2,1)} %param.21) | copy-start | bytes 1572868
  198.6 52.8 %copy-start.6 = (bf16[1,512,512]{2,1,0:T(8,128)(2,1)S(1)}, bf16[1,512,512]{2,1,0:T(8,128)(2,1)}, u32[]{:S(2)}) copy-start(bf16[1,512,512]{2,1,0:T(8,128)(2,1)} %param.22) | copy-start | bytes 1572868
  204.4 3.4 copy-start.1
  215.0 3.4 copy-start.1
  225.6 3.4 copy-start.1
  236.2 3.4 copy-start.1
  243.3 17.7 %all-to-all-start = ((bf16[48,4,512]{2,1,0:T(4,128)(2,1)}), bf16[48,4,512]{2,1,0:T(4,128)(2,1)S(1)}, u32[]{:S(2)}, u32[]{:S(2)}) async-start(bf16[48,4,512]{2,1,0:T(4,128)(2,1)} %reshape.291), calls=%async_computation | async-start | bytes 393216 | tf_op jit(solution)/shard_map/all_to_all | solution.py:170
  251.4 406.1 %all-reduce.7.cloned.1.call-start = ((), (), s32[]{:S(2)}) async-start(), calls=%async_computation.11 | async-start | bytes 2097152 | tf_op jit(solution)/shard_map/psum | solution.py:19
  252.5 408.3 %copy-start.8 = (bf16[512,48]{0,1:T(8,128)(2,1)S(1)}, bf16[512,48]{0,1:T(8,128)(2,1)}, u32[]{:S(2)}) copy-start(bf16[512,48]{0,1:T(8,128)(2,1)} %param.19) | copy-start | bytes 147460
  252.5 408.3 %copy-start.10 = (s32[1,128,1]{1,2,0:T(1,128)S(1)}, s32[1,128,1]{1,2,0:T(1,128)}, u32[]{:S(2)}) copy-start(s32[1,128,1]{1,2,0:T(1,128)} %param.20) | copy-start | bytes 1540
  261.1 400.9 %copy-start.3 = (bf16[1,128,512]{2,1,0:T(8,128)(2,1)S(1)}, bf16[1,128,512]{2,1,0:T(8,128)(2,1)}, u32[]{:S(2)}) copy-start(bf16[1,128,512]{2,1,0:T(8,128)(2,1)} %param.23) | copy-start | bytes 393220
  261.4 6.5 copy-start.7
  262.4 398.7 %all-to-all-start.1 = ((bf16[48,4,512]{2,1,0:T(4,128)(2,1)}), bf16[48,4,512]{2,1,0:T(4,128)(2,1)S(1)}, u32[]{:S(2)}, u32[]{:S(2)}) async-start(bf16[48,4,512]{2,1,0:T(4,128)(2,1)} %reshape.293), calls=%async_computation.1 | async-start | bytes 393216 | tf_op jit(solution)/shard_map/all_to_all | solution.py:177
  267.8 832.2 %all-reduce.5.cloned.1.call-start = ((), (), s32[]{:S(2)}) async-start(), calls=%async_computation.10 | async-start | bytes 4194304 | tf_op jit(solution)/shard_map/psum | solution.py:208
  657.5 5.9 copy-start.5
  668.2 18.3 %all-to-all-start.2 = ((bf16[48,4,512]{2,1,0:T(4,128)(2,1)}), bf16[48,4,512]{2,1,0:T(4,128)(2,1)S(1)}, u32[]{:S(2)}, u32[]{:S(2)}) async-start(bf16[48,4,512]{2,1,0:T(4,128)(2,1)} %reshape.295), calls=%async_computation.2 | async-start | bytes 393216 | tf_op jit(solution)/shard_map/all_to_all | solution.py:171
  676.9 556.1 %reduce-scatter.3.cloned.1.call-start = ((), (), s32[]{:S(2)}) async-start(), calls=%async_computation.8 | async-start | bytes 557056 | tf_op jit(solution)/shard_map/reduce_scatter | solution.py:227
  687.9 424.9 %copy-start.4 = (bf16[512,512]{1,0:T(8,128)(2,1)S(1)}, bf16[512,512]{1,0:T(8,128)(2,1)}, u32[]{:S(2)}) copy-start(bf16[512,512]{1,0:T(8,128)(2,1)} %get-tuple-element.204) | copy-start | bytes 1572868
  1102.3 17.9 %all-to-all-start.3 = ((bf16[48,4,512]{2,1,0:T(4,128)(2,1)}), bf16[48,4,512]{2,1,0:T(4,128)(2,1)S(1)}, u32[]{:S(2)}, u32[]{:S(2)}) async-start(bf16[48,4,512]{2,1,0:T(4,128)(2,1)} %reshape.297), calls=%async_computation.3 | async-start | bytes 393216 | tf_op jit(solution)/shard_map/all_to_all | solution.py:184
  1110.6 229.5 %reduce-scatter.5.cloned.1.call-start = ((), (), s32[]{:S(2)}) async-start(), calls=%async_computation.9 | async-start | bytes 557056 | tf_op jit(solution)/shard_map/reduce_scatter | solution.py:230
Sparse Core Ops, SparseCore 0:
  13.0 96.4 all-gather.2
  113.6 84.9 all-gather.4
  1101.4 131.5 reduce-scatter.2
  1237.4 102.6 reduce-scatter.4
Sparse Core Ops, SparseCore 1:
  255.1 402.3 all-reduce.6
  666.3 433.7 all-reduce.4
where the time goes:
time: 1350 us
  waiting for transfers between devices  1220 us (90%)
  other arithmetic  31.4 us (2%)
  starting transfers between devices  30.9 us (2%)
  matrix products  29 us (2%)
  local copies, waits for them, and re-layouts  19.4 us (1%)
  between operations  16.7 us (1%)
    psum x1, waiting for transfers between devices, local(): summed_in, summed_out = lax.psum((hot_grad_in, hot_grad_out), 'expert')  412 us
    psum x1, waiting for transfers between devices, spread(): return lax.psum(jnp.where(mine, x, jnp.zeros_like(x)), axis)  390 us
    reduce_scatter x1, waiting for transfers between devices, local(): lax.psum_scatter(grad_in_own.astype(jnp.bfloat16), ('seq', 'rep'), scatte...  111 us
    reduce_scatter x1, waiting for transfers between devices, local(): lax.psum_scatter(grad_out_own.astype(jnp.bfloat16), ('seq', 'rep'), scatt...  106 us
    all_gather x1, waiting for transfers between devices, local(): value_part = lax.all_gather(value_rows, ('seq', 'rep'), axis=1, tiled=True)  89.1 us
    all_gather x1, waiting for transfers between devices, local(): key_part = lax.all_gather(key_rows, ('seq', 'rep'), axis=1, tiled=True)  88.4 us
  transfers between devices with their start and end apart: 10, of which 9 were waited for; matrix products, arithmetic and copies ran while one was open for 2% of the time, Pallas kernels for 0%

commit v1 on v0

v1 whole, which is shorter than its diff:
```python
import functools
import math

import jax
import jax.numpy as jnp
from jax import lax
from jax.experimental import pallas as pl
from jax.experimental.pallas import tpu as pltpu
from jax.sharding import PartitionSpec as P

D = 512
H = 16
HD = 32
FF = 512
T = 128
EXPERTS = 48
SLOTS = 16
WINDOW = 1024
norm_eps = 1e-06
masked_score = -1e30
F32 = jnp.float32
BF16 = jnp.bfloat16
VMEM = pl.BlockSpec(memory_space=pltpu.VMEM)


def attention_body(blocks, start_ref, heads_ref, out_ref, q_all, k_all, v_all):
    seq = blocks * T
    for b in range(blocks):
        cols = pl.ds(b * T, T)
        q_all[:, cols] = heads_ref[b, 0:HD, :]
        v_all[:, cols] = heads_ref[b, 2 * HD : 3 * HD, :]
        k_all[cols, :] = heads_ref[b, HD : 2 * HD, :].astype(F32).T.astype(BF16)
    scale = math.log2(math.e) / math.sqrt(HD)
    chunk = 256
    for c in range(seq // chunk):
        first_q = c * chunk
        first_k = max(0, first_q - WINDOW)
        span = first_q + chunk - first_k
        queries = pl.ds(first_q, chunk)
        scores = jnp.dot(
            k_all[pl.ds(first_k, span), :], q_all[:, queries], preferred_element_type=F32
        )
        key_pos = lax.broadcasted_iota(jnp.int32, (span, chunk), 0) + first_k
        query_pos = lax.broadcasted_iota(jnp.int32, (span, chunk), 1) + first_q
        visible = (key_pos >= start_ref[:, queries]) & (key_pos <= query_pos)
        scores = jnp.where(visible, scores, masked_score)
        top = jnp.max(scores, axis=0, keepdims=True)
        weights = jnp.exp2((scores - top) * scale)
        totals = jnp.sum(weights, axis=0, keepdims=True)
        result = jnp.dot(
            v_all[:, pl.ds(first_k, span)], weights.astype(BF16), preferred_element_type=F32
        )
        result = (result / totals).astype(BF16)
        for j in range(chunk // T):
            out_ref[c * (chunk // T) + j] = result[:, j * T : (j + 1) * T]


def attention(heads, start):
    blocks = heads.shape[0]
    seq = blocks * T
    return pl.pallas_call(
        functools.partial(attention_body, blocks),
        out_shape=jax.ShapeDtypeStruct((blocks, HD, T), BF16),
        in_specs=[VMEM, VMEM],
        out_specs=VMEM,
        scratch_shapes=[
            pltpu.VMEM((HD, seq), BF16),
            pltpu.VMEM((seq, HD), BF16),
            pltpu.VMEM((HD, seq), BF16),
        ],
        cost_estimate=pl.CostEstimate(flops=300000000, bytes_accessed=600000, transcendentals=2000000),
        name="attention",
    )(start, heads)


def slots_row(chosen_row, experts, slots):
    ids = lax.broadcasted_iota(jnp.int32, (experts, T), 0)
    hits = chosen_row == ids
    before = lax.broadcasted_iota(jnp.int32, (T, T), 0) < lax.broadcasted_iota(
        jnp.int32, (T, T), 1
    )
    ranks = jnp.dot(
        hits.astype(F32).astype(BF16), before.astype(F32).astype(BF16), preferred_element_type=F32
    )
    rank = jnp.sum(jnp.where(hits, ranks, 0.0), axis=0, keepdims=True)
    return chosen_row * slots + rank.astype(jnp.int32)


def slots_column(hits, chosen_col, slots):
    before = lax.broadcasted_iota(jnp.int32, (T, T), 1) < lax.broadcasted_iota(
        jnp.int32, (T, T), 0
    )
    ranks = jnp.dot(
        before.astype(F32).astype(BF16), hits.astype(F32).astype(BF16), preferred_element_type=F32
    )
    rank = jnp.sum(jnp.where(hits, ranks, 0.0), axis=1, keepdims=True)
    return chosen_col * slots + rank.astype(jnp.int32)


def mix_body(
    experts, att_ref, residual_ref, proj_ref, router_ref, row_ref, col_ref, grad_ref,
    mixed_ref, stats_ref, send_ref,
):
    attended = att_ref[...].astype(F32).T.astype(BF16)
    mixed = (
        residual_ref[...].astype(F32)
        + jnp.dot(attended, proj_ref[...], preferred_element_type=F32)
    ).astype(BF16)
    mixed_ref[...] = mixed
    mixed_f = mixed.astype(F32)
    inv_rms = lax.rsqrt(jnp.mean(mixed_f * mixed_f, axis=1, keepdims=True) + norm_eps)
    normed = (mixed_f * inv_rms).astype(BF16)
    logits = jnp.dot(normed, router_ref[...], preferred_element_type=F32)
    hits = col_ref[...] == lax.broadcasted_iota(jnp.int32, (T, experts), 1)
    gate = jax.nn.sigmoid(jnp.sum(jnp.where(hits, logits, 0.0), axis=1, keepdims=True))
    scaled = (gate * grad_ref[...].astype(F32)).astype(BF16)
    stats_ref[...] = jnp.concatenate(
        [jnp.broadcast_to(inv_rms, (T, T)), jnp.broadcast_to(gate, (T, T))], axis=1
    )
    slot = slots_row(row_ref[...], experts, SLOTS)
    place = lax.broadcasted_iota(jnp.int32, (experts * SLOTS, T), 0) == slot
    place = place.astype(F32).astype(BF16)
    send_ref[:, 0:D] = jnp.dot(place, normed, preferred_element_type=F32).astype(BF16)
    send_ref[:, D : 2 * D] = jnp.dot(place, scaled, preferred_element_type=F32).astype(BF16)


def final_body(
    experts, back_ref, mixed_ref, stats_ref, router_ref, col_ref, grad_ref, out_ref, grad_mixed_ref
):
    chosen = col_ref[...]
    hits = chosen == lax.broadcasted_iota(jnp.int32, (T, experts), 1)
    slot = slots_column(hits, chosen, SLOTS)
    pick = lax.broadcasted_iota(jnp.int32, (T, experts * SLOTS), 1) == slot
    pick = pick.astype(F32).astype(BF16)
    result_f = jnp.dot(pick, back_ref[:, 0:D], preferred_element_type=F32)
    normed_grad = jnp.dot(pick, back_ref[:, D : 2 * D], preferred_element_type=F32)
    mixed_f = mixed_ref[...].astype(F32)
    inv_rms = stats_ref[:, 0:1]
    gate = stats_ref[:, T : T + 1]
    grad_f = grad_ref[...].astype(F32)
    out_ref[...] = (mixed_f + gate * result_f).astype(BF16)
    gate_grad = jnp.sum(grad_f * result_f, axis=1, keepdims=True)
    logit_grad = gate_grad * gate * (1.0 - gate)
    router_cols = lax.dot_general(
        hits.astype(F32).astype(BF16), router_ref[...], (((1,), (1,)), ((), ())),
        preferred_element_type=F32,
    )
    total_grad = normed_grad + logit_grad * router_cols
    mean_term = jnp.mean(total_grad * mixed_f, axis=1, keepdims=True)
    input_grad = inv_rms * total_grad - mixed_f * inv_rms * inv_rms * inv_rms * mean_term
    grad_mixed_ref[...] = (grad_f + input_grad).astype(BF16)


def expert_body(rows_ref, up_ref, down_ref, back_ref, grads_ref, act_ref, pre_ref):
    up = up_ref[...]
    down = down_ref[...]
    rows = rows_ref.shape[0]
    step = 256
    contract_last = (((1,), (1,)), ((), ()))
    contract_first = (((0,), (0,)), ((), ()))

    def block(i, carry):
        here = pl.ds(pl.multiple_of(i * step, step), step)
        tokens = rows_ref[here, 0:D]
        grads = rows_ref[here, D : 2 * D]
        pre = jnp.dot(tokens, up, preferred_element_type=F32)
        sig = jax.nn.sigmoid(pre)
        activated = (pre * sig).astype(BF16)
        back_ref[here, 0:D] = jnp.dot(activated, down, preferred_element_type=F32).astype(BF16)
        act_grad = lax.dot_general(grads, down, contract_last, preferred_element_type=F32)
        pre_grad = (act_grad * sig * (1.0 + pre * (1.0 - sig))).astype(BF16)
        back_ref[here, D : 2 * D] = lax.dot_general(
            pre_grad, up, contract_last, preferred_element_type=F32
        ).astype(BF16)
        act_ref[here, :] = activated
        pre_ref[here, :] = pre_grad
        return carry

    lax.fori_loop(0, rows // step, block, 0)
    grad_up = lax.dot_general(
        rows_ref[:, 0:D], pre_ref[...], contract_first, preferred_element_type=F32
    )
    grads_ref[:, 0:FF] = grad_up.astype(BF16)
    grad_down = lax.dot_general(
        act_ref[...], rows_ref[:, D : 2 * D], contract_first, preferred_element_type=F32
    )
    grads_ref[:, FF : FF + D] = grad_down.astype(BF16)


def sum_body(parts, got_ref, in_ref, out_ref):
    total = got_ref[0].astype(F32)
    for p in range(1, parts):
        total = total + got_ref[p].astype(F32)
    in_ref[...] = total[:, 0:FF]
    out_ref[...] = total[:, FF : FF + D]


def local(
    query_rows, key_rows, value_rows, doc_lengths, residual, out_proj, router, expert_choice,
    weight_in, weight_out, grad_out,
):
    ranks = lax.axis_size(("seq", "rep"))
    experts = router.shape[1]
    seq = ranks * T
    group = ("seq", "rep")
    heads = jnp.concatenate(
        [
            query_rows[0].T.reshape(H, HD, T),
            key_rows[0].T.reshape(H, HD, T),
            value_rows[0].T.reshape(H, HD, T),
        ],
        axis=1,
    )
    heads = lax.all_to_all(heads, group, split_axis=0, concat_axis=0, tiled=True)
    boundaries = jnp.cumsum(doc_lengths[0])[:-1]
    positions = jnp.arange(seq, dtype=jnp.int32)
    start = jnp.max(
        jnp.where(positions[None, :] >= boundaries[:, None], boundaries[:, None], 0),
        axis=0,
        keepdims=True,
    )
    attended = attention(heads, start)
    attended = lax.all_to_all(attended, group, split_axis=0, concat_axis=0, tiled=True)
    chosen_col = expert_choice[0]
    chosen_row = chosen_col.reshape(1, T)
    grad_rows = grad_out[0]
    mixed, stats, send = pl.pallas_call(
        functools.partial(mix_body, experts),
        out_shape=(
            jax.ShapeDtypeStruct((T, D), BF16),
            jax.ShapeDtypeStruct((T, 2 * T), F32),
            jax.ShapeDtypeStruct((experts * SLOTS, 2 * D), BF16),
        ),
        in_specs=[VMEM] * 7,
        out_specs=(VMEM,) * 3,
        name="mix",
    )(attended.reshape(D, T), residual[0], out_proj, router, chosen_row, chosen_col, grad_rows)
    got = lax.all_to_all(
        send.reshape(experts, SLOTS, 2 * D), "expert", split_axis=0, concat_axis=0, tiled=True
    )
    back, grads = pl.pallas_call(
        expert_body,
        out_shape=(
            jax.ShapeDtypeStruct((experts * SLOTS, 2 * D), BF16),
            jax.ShapeDtypeStruct((D, FF + D), BF16),
        ),
        in_specs=[VMEM] * 3,
        out_specs=(VMEM,) * 2,
        scratch_shapes=[
            pltpu.VMEM((experts * SLOTS, FF), BF16),
            pltpu.VMEM((experts * SLOTS, FF), BF16),
        ],
        cost_estimate=pl.CostEstimate(flops=2400000000, bytes_accessed=5000000, transcendentals=400000),
        name="expert",
    )(got.reshape(experts * SLOTS, 2 * D), weight_in[0], weight_out[0])
    back = lax.all_to_all(
        back.reshape(experts, SLOTS, 2 * D), "expert", split_axis=0, concat_axis=0, tiled=True
    )
    shares = lax.all_to_all(
        grads.reshape(ranks, D // ranks, FF + D), group, split_axis=0, concat_axis=0, tiled=True
    )
    share_in, share_out = pl.pallas_call(
        functools.partial(sum_body, ranks),
        out_shape=(jax.ShapeDtypeStruct((D // ranks, FF), F32),) * 2,
        in_specs=[VMEM],
        out_specs=(VMEM,) * 2,
        name="grad_sum",
    )(shares)
    layer_out, grad_mixed = pl.pallas_call(
        functools.partial(final_body, experts),
        out_shape=(jax.ShapeDtypeStruct((T, D), BF16),) * 2,
        in_specs=[VMEM] * 6,
        out_specs=(VMEM,) * 2,
        name="final",
    )(back.reshape(experts * SLOTS, 2 * D), mixed, stats, router, chosen_col, grad_rows)
    return (layer_out[None], grad_mixed[None], share_in[None], share_out[None])


def solution(mesh):
    rows = P("expert", ("seq", "rep"), None)
    weights = P("expert", None, None)
    in_specs = (
        rows, rows, rows, P("expert", None), rows, P(), P(), rows, weights, weights, rows,
    )
    return jax.shard_map(
        local, mesh=mesh, in_specs=in_specs, out_specs=(rows,) * 4, check_vma=False
    )
```

time: 1350 us -> 226 us (0.17)
  waiting for transfers between devices: 1220 us -> 60 us
  blocking collectives: 0 us -> 87.5 us
  other arithmetic: 31.4 us -> 1.66 us
  matrix products: 29 us -> 0 us
  Pallas kernels: 0 us -> 22.1 us
  between operations: 16.7 us -> 0.71 us
  starting transfers between devices: 30.9 us -> 45.6 us
    psum x2 -> x0, waiting for transfers between devices: 802 us -> none  [the longest x1 412 us: local(): summed_in, summed_out = lax.psum((hot_grad_in, hot_grad_out), 'expert')]
    reduce_scatter x2 -> x0, waiting for transfers between devices: 216 us -> none  [the longest x1 111 us: local(): lax.psum_scatter(grad_in_own.astype(jnp.bfloat16), ('seq', 'rep'), scatte...]
    all_gather x2 -> x0, waiting for transfers between devices: 177 us -> none  [the longest x1 89.1 us: local(): value_part = lax.all_gather(value_rows, ('seq', 'rep'), axis=1, tiled=True)]
    all_to_all x0 -> x2, blocking collectives: none -> 87.5 us  [the longest x1 54.8 us: local(): lax.all_to_all(send.reshape(experts, SLOTS, 2 * D), 'expert', split_axis=...]
    all_to_all x4 -> x3, waiting for transfers between devices: 22.5 us -> 60 us  [the longest x1 37.3 us: local(): lax.all_to_all(back.reshape(experts, SLOTS, 2 * D), 'expert', split_axis=...]
    dot_general x23 -> x0, matrix products: 29 us -> none  [the longest x4 11.6 us: attend_fold(): jnp.einsum('qhd,khd->hqk', query_heads, key_heads, preferred_element_type...]
    pallas_call x0 -> x5, Pallas kernels: none -> 22.1 us  [the longest x1 6.78 us: attention(): pl.pallas_call(functools.partial(attention_body, blocks), out_shape=jax.S...]
    reduce_sum x13 -> x0, other arithmetic: 16 us -> none  [the longest x4 13.3 us: attend_fold(): totals = totals * factor + jnp.sum(weights, axis=2)]
  transfers between devices with their start and end apart: 10 -> 3, of which waited for: 9 -> 3; matrix products, arithmetic and copies ran while one was open for 2% -> 1% of each run, Pallas kernels for 0% -> 1%
where the time goes in v1:
time: 226 us; the launch traced here: 225 us
  blocking collectives  87.5 us (39%)
  waiting for transfers between devices  60 us (27%)
  starting transfers between devices  45.6 us (20%)
  Pallas kernels  22.1 us (10%)
  local copies, waits for them, and re-layouts  7.12 us (3%)
    all_to_all x1, blocking collectives, local(): lax.all_to_all(send.reshape(experts, SLOTS, 2 * D), 'expert', split_axis=...  54.8 us
    all_to_all x1, waiting for transfers between devices, local(): lax.all_to_all(back.reshape(experts, SLOTS, 2 * D), 'expert', split_axis=...  37.3 us
    all_to_all x1, blocking collectives, local(): lax.all_to_all(grads.reshape(ranks, D // ranks, FF + D), group, split_axi...  32.7 us
    all_to_all x1, starting transfers between devices, local(): lax.all_to_all(back.reshape(experts, SLOTS, 2 * D), 'expert', split_axis=...  20.6 us
    all_to_all x1, starting transfers between devices, local(): lax.all_to_all(heads, group, split_axis=0, concat_axis=0, tiled=True)  17.6 us
    all_to_all x1, waiting for transfers between devices, local(): lax.all_to_all(heads, group, split_axis=0, concat_axis=0, tiled=True)  12.7 us
    all_to_all x1, waiting for transfers between devices, local(): lax.all_to_all(attended, group, split_axis=0, concat_axis=0, tiled=True)  10 us
    all_to_all x1, starting transfers between devices, local(): lax.all_to_all(attended, group, split_axis=0, concat_axis=0, tiled=True)  7.46 us
  transfers between devices with their start and end apart: 3, of which 3 were waited for; matrix products, arithmetic and copies ran while one was open for 1% of the time, Pallas kernels for 1%

profile of v1, /device:TPU:1, one launch (start us, length us, event | category | flops | bytes accessed | tf_op | source)
XLA Modules:
  0.0 224.7 jit_solution(18277627804073848764)
XLA Ops:
  0.6 0.0 copy-start.5
  0.6 1.0 copy.22
  1.7 1.0 copy.23
  2.7 1.0 copy.24
  3.7 0.8 pad_maximum_fusion
  4.5 17.6 %all-to-all-start = ((bf16[16,96,128]{2,1,0:T(8,128)(2,1)}), bf16[16,96,128]{2,1,0:T(8,128)(2,1)S(1)}, u32[]{:S(2)}, u32[]{:S(2)}) async-start(bf16[16,96,128]{2,1,0:T(8,128)(2,1)} %pad_maximum_fusion), calls=%async_computation | async-start | bytes 786432 | tf_op jit(solution)/shard_map/all_to_all | solution.py:214
  22.1 0.0 copy-done.5
  22.1 0.2 reduce-window.4
  22.3 0.7 select_reduce_fusion
  23.0 12.7 %all-to-all-done.heads_ref = bf16[16,96,128]{2,1,0:T(8,128)(2,1)S(1)} async-done(((bf16[16,96,128]{2,1,0:T(8,128)(2,1)}), bf16[16,96,128]{2,1,0:T(8,128)(2,1)S(1)}, u32[]{:S(2)}, u32[]{:S(2)}) %all-to-all-start) | async-done | bytes 393248 | tf_op jit(solution)/shard_map/all_to_all | solution.py:214
  35.7 0.0 copy-start.2
  35.7 0.7 copy-done.2
  36.4 0.0 copy-start.4
  36.5 0.0 copy-start.3
  36.5 6.8 %attention.1 = bf16[16,32,128]{2,1,0:T(8,128)(2,1)} custom-call(s32[1,2048]{1,0:T(1,128)} %bitcast.46, bf16[16,96,128]{2,1,0:T(8,128)(2,1)} %copy-done.2), custom_call_target="tpu_custom_call" | custom-call | flops 300000000 | bytes 600000 | tf_op jit(solution)/shard_map/attention/pallas_call | solution.py:61
  43.2 7.5 %all-to-all-start.1 = ((bf16[16,32,128]{2,1,0:T(8,128)(2,1)}), bf16[16,32,128]{2,1,0:T(8,128)(2,1)S(1)}, u32[]{:S(2)}, u32[]{:S(2)}) async-start(bf16[16,32,128]{2,1,0:T(8,128)(2,1)} %attention.1), calls=%async_computation.1 | async-start | bytes 262144 | tf_op jit(solution)/shard_map/all_to_all | solution.py:223
  50.7 0.0 copy-done.4
  50.7 0.7 copy.26.col_ref
  51.4 0.0 copy-done.3
  51.4 0.7 copy.25.router_ref
  52.2 10.0 %all-to-all-done.1 = bf16[16,32,128]{2,1,0:T(8,128)(2,1)S(1)} async-done(((bf16[16,32,128]{2,1,0:T(8,128)(2,1)}), bf16[16,32,128]{2,1,0:T(8,128)(2,1)S(1)}, u32[]{:S(2)}, u32[]{:S(2)}) %all-to-all-start.1) | async-done | bytes 131104 | tf_op jit(solution)/shard_map/all_to_all | solution.py:223
  62.2 0.0 copy-start.1
  62.2 0.7 copy-done.1
  62.9 3.6 %mix.1 = (bf16[128,512]{1,0:T(8,128)(2,1)}, f32[128,256]{1,0:T(8,128)}, bf16[768,1024]{1,0:T(8,128)(2,1)}) custom-call(bf16[512,128]{1,0:T(8,128)(2,1)} %bitcast.41, bf16[128,512]{1,0:T(8,128)(2,1)} %bitcast.45, bf16[512,512]{1,0:T(8,128)(2,1)} %proj_ref.1, bf16[512,48]{1,0:T(8,128)(2,1)} %copy.25.router_ref, s32[1,128]{1,0:T(1,128)} %bitcast.47, ...), custom_call_target="tpu_custom_call" | custom-call | tf_op jit(solution)/shard_map/mix/pallas_call | solution.py:227
  66.4 54.8 %all_to_all.25 = bf16[48,16,1024]{2,1,0:T(8,128)(2,1)} all-to-all(bf16[48,16,1024]{2,1,0:T(8,128)(2,1)} %bitcast.33), channel_id=1, replica_groups=mesh['seq'=4,'expert'=48,'rep'=4] {'expert'}, dimensions={0} | all-to-all | bytes 3145728 | tf_op jit(solution)/shard_map/all_to_all | solution.py:238
  121.3 6.6 %expert.1 = (bf16[768,1024]{1,0:T(8,128)(2,1)}, bf16[512,1024]{1,0:T(8,128)(2,1)}) custom-call(bf16[768,1024]{1,0:T(8,128)(2,1)} %bitcast.34, bf16[512,512]{1,0:T(8,128)(2,1)} %bitcast.49, bf16[512,512]{1,0:T(8,128)(2,1)} %bitcast.50), custom_call_target="tpu_custom_call" | custom-call | flops 2400000000 | bytes 5000000 | tf_op jit(solution)/shard_map/expert/pallas_call | solution.py:241
  127.9 32.7 %all_to_all.26.got_ref = bf16[16,32,1024]{2,1,0:T(8,128)(2,1)} all-to-all(bf16[16,32,1024]{2,1,0:T(8,128)(2,1)} %bitcast.35), channel_id=1, replica_groups=mesh['seq'=4,'expert'=48,'rep'=4] {'seq','rep'}, dimensions={0} | all-to-all | bytes 2097152 | tf_op jit(solution)/shard_map/all_to_all | solution.py:259
  160.6 20.6 %all-to-all-start.3 = ((bf16[48,16,1024]{2,1,0:T(8,128)(2,1)}), bf16[48,16,1024]{2,1,0:T(8,128)(2,1)S(1)}, u32[]{:S(2)}, u32[]{:S(2)}) async-start(bf16[48,16,1024]{2,1,0:T(8,128)(2,1)} %bitcast.21), calls=%async_computation.3 | async-start | bytes 3145728 | tf_op jit(solution)/shard_map/all_to_all | solution.py:256
  181.2 2.0 grad_sum.1
  183.1 37.3 %all-to-all-done.3 = bf16[48,16,1024]{2,1,0:T(8,128)(2,1)S(1)} async-done(((bf16[48,16,1024]{2,1,0:T(8,128)(2,1)}), bf16[48,16,1024]{2,1,0:T(8,128)(2,1)S(1)}, u32[]{:S(2)}, u32[]{:S(2)}) %all-to-all-start.3) | async-done | bytes 1572896 | tf_op jit(solution)/shard_map/all_to_all | solution.py:256
  220.5 0.0 copy-start
  220.5 1.1 copy-done
  221.6 3.1 %final.1 = (bf16[128,512]{1,0:T(8,128)(2,1)}, bf16[128,512]{1,0:T(8,128)(2,1)}) custom-call(bf16[768,1024]{1,0:T(8,128)(2,1)} %bitcast.32, bf16[128,512]{1,0:T(8,128)(2,1)} %get-tuple-element.15.mixed_ref, f32[128,256]{1,0:T(8,128)} %get-tuple-element.16.stats_ref, bf16[512,48]{1,0:T(8,128)(2,1)} %copy.25.router_ref, s32[128,1]{1,0:T(8,128)} %copy.26.col_ref, ...), custom_call_target="tpu_custom_call" | custom-call | tf_op jit(solution)/shard_map/final/pallas_call | solution.py:269
  (1 shorter events, 0.0 us)
Async XLA Ops:
  0.6 21.5 %copy-start.5 = (s32[1,8]{1,0:T(1,128)S(1)}, s32[1,8]{1,0:T(1,128)}, u32[]{:S(2)}) copy-start(s32[1,8]{1,0:T(1,128)} %param.14) | copy-start | bytes 100
  4.5 31.2 %all-to-all-start = ((bf16[16,96,128]{2,1,0:T(8,128)(2,1)}), bf16[16,96,128]{2,1,0:T(8,128)(2,1)S(1)}, u32[]{:S(2)}, u32[]{:S(2)}) async-start(bf16[16,96,128]{2,1,0:T(8,128)(2,1)} %pad_maximum_fusion), calls=%async_computation | async-start | bytes 786432 | tf_op jit(solution)/shard_map/all_to_all | solution.py:214
  35.7 0.7 copy-start.2
  36.4 14.3 %copy-start.4 = (s32[1,128,1]{1,2,0:T(1,128)S(1)}, s32[1,128,1]{1,2,0:T(1,128)}, u32[]{:S(2)}) copy-start(s32[1,128,1]{1,2,0:T(1,128)} %param.18) | copy-start | bytes 1540
  36.5 15.0 %copy-start.3 = (bf16[512,48]{0,1:T(8,128)(2,1)S(1)}, bf16[512,48]{0,1:T(8,128)(2,1)}, u32[]{:S(2)}) copy-start(bf16[512,48]{0,1:T(8,128)(2,1)} %param.17) | copy-start | bytes 147460
  43.2 19.0 %all-to-all-start.1 = ((bf16[16,32,128]{2,1,0:T(8,128)(2,1)}), bf16[16,32,128]{2,1,0:T(8,128)(2,1)S(1)}, u32[]{:S(2)}, u32[]{:S(2)}) async-start(bf16[16,32,128]{2,1,0:T(8,128)(2,1)} %attention.1), calls=%async_computation.1 | async-start | bytes 262144 | tf_op jit(solution)/shard_map/all_to_all | solution.py:223
  62.2 0.7 copy-start.1
  160.6 59.9 %all-to-all-start.3 = ((bf16[48,16,1024]{2,1,0:T(8,128)(2,1)}), bf16[48,16,1024]{2,1,0:T(8,128)(2,1)S(1)}, u32[]{:S(2)}, u32[]{:S(2)}) async-start(bf16[48,16,1024]{2,1,0:T(8,128)(2,1)} %bitcast.21), calls=%async_computation.3 | async-start | bytes 3145728 | tf_op jit(solution)/shard_map/all_to_all | solution.py:256
  220.5 1.2 copy-start

commit v2 on v1

v2 whole, which is shorter than its diff:
```python
import functools
import math

import jax
import jax.numpy as jnp
from jax import lax
from jax.experimental import pallas as pl
from jax.experimental.pallas import tpu as pltpu
from jax.sharding import PartitionSpec as P

D = 512
H = 16
HD = 32
FF = 512
T = 128
EXPERTS = 48
SLOTS = 16
WINDOW = 1024
CHUNK = 256
MESH = pl.DeviceIdType.MESH
norm_eps = 1e-06
masked_score = -1e30
F32 = jnp.float32
BF16 = jnp.bfloat16
VMEM = pl.BlockSpec(memory_space=pltpu.VMEM)


def group_device(rank, reps):
    return {"seq": rank // reps, "rep": lax.rem(rank, reps)}


def attend_chunk(c, start, q_all, k_all, v_all):
    scale = math.log2(math.e) / math.sqrt(HD)
    first_q = c * CHUNK
    first_k = max(0, first_q - WINDOW)
    span = first_q + CHUNK - first_k
    queries = pl.ds(first_q, CHUNK)
    scores = jnp.dot(
        k_all[pl.ds(first_k, span), :], q_all[:, queries], preferred_element_type=F32
    )
    key_pos = lax.broadcasted_iota(jnp.int32, (span, CHUNK), 0) + first_k
    query_pos = lax.broadcasted_iota(jnp.int32, (span, CHUNK), 1) + first_q
    visible = (key_pos >= start) & (key_pos <= query_pos)
    scores = jnp.where(visible, scores, masked_score)
    top = jnp.max(scores, axis=0, keepdims=True)
    weights = jnp.exp2((scores - top) * scale)
    totals = jnp.sum(weights, axis=0, keepdims=True)
    result = jnp.dot(
        v_all[:, pl.ds(first_k, span)], weights.astype(BF16), preferred_element_type=F32
    )
    return (result / totals).astype(BF16)


def attend_body(
    blocks, reps, experts, lengths_ref, query_ref, key_ref, value_ref, residual_ref, proj_ref,
    router_ref, row_ref, col_ref, grad_ref, mixed_ref, stats_ref, send_ref,
    heads, got, result, att, q_all, k_all, v_all,
    send_sem, recv_sem, back_send_sem, back_recv_sem,
):
    me = lax.axis_index("seq") * reps + lax.axis_index("rep")
    barrier = pltpu.get_barrier_semaphore()

    def greet(k, carry):
        pl.semaphore_signal(
            barrier, inc=1, device_id=group_device(lax.rem(me + k, blocks), reps),
            device_id_type=MESH,
        )
        return carry

    lax.fori_loop(1, blocks, greet, 0)
    for i, ref in enumerate((query_ref, key_ref, value_ref)):
        flipped = ref[...].astype(F32).T.astype(BF16)
        for h in range(blocks):
            heads[h, i * HD : (i + 1) * HD, :] = flipped[h * HD : (h + 1) * HD]
    starts = []
    for c in range(blocks * T // CHUNK):
        pos = lax.broadcasted_iota(jnp.int32, (1, CHUNK), 1) + c * CHUNK
        edge = jnp.int32(0)
        start = jnp.zeros((1, CHUNK), jnp.int32)
        for d in range(lengths_ref.shape[1] - 1):
            edge = edge + lengths_ref[0, d]
            start = jnp.where(pos >= edge, edge, start)
        starts.append(start)
    pl.semaphore_wait(barrier, blocks - 1)

    def outgoing(k):
        to = lax.rem(me + k, blocks)
        return pltpu.make_async_remote_copy(
            src_ref=heads.at[to], dst_ref=got.at[me], send_sem=send_sem.at[to],
            recv_sem=recv_sem.at[me], device_id=group_device(to, reps), device_id_type=MESH,
        )

    def launch(k, carry):
        outgoing(k).start()
        return carry

    lax.fori_loop(1, blocks, launch, 0)
    got[me] = heads[me]

    def incoming(b):
        return pltpu.make_async_remote_copy(
            src_ref=heads.at[b], dst_ref=got.at[b], send_sem=send_sem.at[b],
            recv_sem=recv_sem.at[b], device_id=group_device(b, reps), device_id_type=MESH,
        )

    def returning(b):
        return pltpu.make_async_remote_copy(
            src_ref=result.at[b], dst_ref=att.at[me], send_sem=back_send_sem.at[b],
            recv_sem=back_recv_sem.at[me], device_id=group_device(b, reps), device_id_type=MESH,
        )

    per = CHUNK // T

    def give_back(c):
        for b in range(c * per, (c + 1) * per):

            @pl.when(me != b)
            def _():
                returning(b).start()

            @pl.when(me == b)
            def _():
                att[b] = result[b]

    chunks = blocks // per
    for c in range(chunks):
        for b in range(c * per, (c + 1) * per):

            @pl.when(me != b)
            def _():
                incoming(b).wait_recv()

            cols = pl.ds(b * T, T)
            q_all[:, cols] = got[b, 0:HD, :]
            v_all[:, cols] = got[b, 2 * HD : 3 * HD, :]
            k_all[cols, :] = got[b, HD : 2 * HD, :].astype(F32).T.astype(BF16)
        done = attend_chunk(c, starts[c], q_all, k_all, v_all)
        for j in range(per):
            result[c * per + j] = done[:, j * T : (j + 1) * T]
        if c:
            give_back(c - 1)
    slot = slots_row(row_ref[...], experts, SLOTS)
    place = lax.broadcasted_iota(jnp.int32, (experts * SLOTS, T), 0) == slot
    place = place.astype(F32).astype(BF16)
    give_back(chunks - 1)

    def arrived(k, carry):
        b = lax.rem(me + k, blocks)
        pltpu.make_async_remote_copy(
            src_ref=result.at[b], dst_ref=att.at[b], send_sem=back_send_sem.at[b],
            recv_sem=back_recv_sem.at[b], device_id=group_device(b, reps), device_id_type=MESH,
        ).wait_recv()
        return carry

    lax.fori_loop(1, blocks, arrived, 0)
    attended = att[...].reshape(D, T).astype(F32).T.astype(BF16)
    mixed = (
        residual_ref[...].astype(F32)
        + jnp.dot(attended, proj_ref[...], preferred_element_type=F32)
    ).astype(BF16)
    mixed_ref[...] = mixed
    mixed_f = mixed.astype(F32)
    inv_rms = lax.rsqrt(jnp.mean(mixed_f * mixed_f, axis=1, keepdims=True) + norm_eps)
    normed = (mixed_f * inv_rms).astype(BF16)
    logits = jnp.dot(normed, router_ref[...], preferred_element_type=F32)
    hits = col_ref[...] == lax.broadcasted_iota(jnp.int32, (T, experts), 1)
    gate = jax.nn.sigmoid(jnp.sum(jnp.where(hits, logits, 0.0), axis=1, keepdims=True))
    scaled = (gate * grad_ref[...].astype(F32)).astype(BF16)
    stats_ref[...] = jnp.concatenate(
        [jnp.broadcast_to(inv_rms, (T, T)), jnp.broadcast_to(gate, (T, T))], axis=1
    )
    send_ref[:, 0:D] = jnp.dot(place, normed, preferred_element_type=F32).astype(BF16)
    send_ref[:, D : 2 * D] = jnp.dot(place, scaled, preferred_element_type=F32).astype(BF16)

    def finish(k, carry):
        outgoing(k).wait_send()
        returning(lax.rem(me + k, blocks)).wait_send()
        return carry

    lax.fori_loop(1, blocks, finish, 0)


def slots_row(chosen_row, experts, slots):
    ids = lax.broadcasted_iota(jnp.int32, (experts, T), 0)
    hits = chosen_row == ids
    before = lax.broadcasted_iota(jnp.int32, (T, T), 0) < lax.broadcasted_iota(
        jnp.int32, (T, T), 1
    )
    ranks = jnp.dot(
        hits.astype(F32).astype(BF16), before.astype(F32).astype(BF16), preferred_element_type=F32
    )
    rank = jnp.sum(jnp.where(hits, ranks, 0.0), axis=0, keepdims=True)
    return chosen_row * slots + rank.astype(jnp.int32)


def slots_column(hits, chosen_col, slots):
    before = lax.broadcasted_iota(jnp.int32, (T, T), 1) < lax.broadcasted_iota(
        jnp.int32, (T, T), 0
    )
    ranks = jnp.dot(
        before.astype(F32).astype(BF16), hits.astype(F32).astype(BF16), preferred_element_type=F32
    )
    rank = jnp.sum(jnp.where(hits, ranks, 0.0), axis=1, keepdims=True)
    return chosen_col * slots + rank.astype(jnp.int32)


def final_body(
    experts, back_ref, mixed_ref, stats_ref, router_ref, col_ref, grad_ref, out_ref, grad_mixed_ref
):
    chosen = col_ref[...]
    hits = chosen == lax.broadcasted_iota(jnp.int32, (T, experts), 1)
    slot = slots_column(hits, chosen, SLOTS)
    pick = lax.broadcasted_iota(jnp.int32, (T, experts * SLOTS), 1) == slot
    pick = pick.astype(F32).astype(BF16)
    result_f = jnp.dot(pick, back_ref[:, 0:D], preferred_element_type=F32)
    normed_grad = jnp.dot(pick, back_ref[:, D : 2 * D], preferred_element_type=F32)
    mixed_f = mixed_ref[...].astype(F32)
    inv_rms = stats_ref[:, 0:1]
    gate = stats_ref[:, T : T + 1]
    grad_f = grad_ref[...].astype(F32)
    out_ref[...] = (mixed_f + gate * result_f).astype(BF16)
    gate_grad = jnp.sum(grad_f * result_f, axis=1, keepdims=True)
    logit_grad = gate_grad * gate * (1.0 - gate)
    router_cols = lax.dot_general(
        hits.astype(F32).astype(BF16), router_ref[...], (((1,), (1,)), ((), ())),
        preferred_element_type=F32,
    )
    total_grad = normed_grad + logit_grad * router_cols
    mean_term = jnp.mean(total_grad * mixed_f, axis=1, keepdims=True)
    input_grad = inv_rms * total_grad - mixed_f * inv_rms * inv_rms * inv_rms * mean_term
    grad_mixed_ref[...] = (grad_f + input_grad).astype(BF16)


def expert_body(rows_ref, up_ref, down_ref, back_ref, grads_ref, act_ref, pre_ref):
    up = up_ref[...]
    down = down_ref[...]
    rows = rows_ref.shape[0]
    step = 256
    contract_last = (((1,), (1,)), ((), ()))
    contract_first = (((0,), (0,)), ((), ()))

    def block(i, carry):
        here = pl.ds(pl.multiple_of(i * step, step), step)
        tokens = rows_ref[here, 0:D]
        grads = rows_ref[here, D : 2 * D]
        pre = jnp.dot(tokens, up, preferred_element_type=F32)
        sig = jax.nn.sigmoid(pre)
        activated = (pre * sig).astype(BF16)
        back_ref[here, 0:D] = jnp.dot(activated, down, preferred_element_type=F32).astype(BF16)
        act_grad = lax.dot_general(grads, down, contract_last, preferred_element_type=F32)
        pre_grad = (act_grad * sig * (1.0 + pre * (1.0 - sig))).astype(BF16)
        back_ref[here, D : 2 * D] = lax.dot_general(
            pre_grad, up, contract_last, preferred_element_type=F32
        ).astype(BF16)
        act_ref[here, :] = activated
        pre_ref[here, :] = pre_grad
        return carry

    lax.fori_loop(0, rows // step, block, 0)
    reps = grads_ref.shape[1]
    share = grads_ref.shape[3]
    grad_up = lax.dot_general(
        rows_ref[:, 0:D], pre_ref[...], contract_first, preferred_element_type=F32
    )
    grad_down = lax.dot_general(
        act_ref[...], rows_ref[:, D : 2 * D], contract_first, preferred_element_type=F32
    )
    for m, grad in enumerate((grad_up, grad_down)):
        for j in range(D // share):
            piece = grad[j * share : (j + 1) * share]
            grads_ref[m, j % reps, j // reps] = piece.astype(BF16)


def reduce_body(
    seqs, reps, grads_ref, in_ref, out_ref, got_x, part, got_z,
    x_send, x_recv, z_send, z_recv,
):
    my_seq = lax.axis_index("seq")
    my_rep = lax.axis_index("rep")
    barrier = pltpu.get_barrier_semaphore()
    for k in range(1, reps):
        pl.semaphore_signal(
            barrier, inc=1, device_id={"rep": lax.rem(my_rep + k, reps)}, device_id_type=MESH
        )
    for k in range(1, seqs):
        pl.semaphore_signal(
            barrier, inc=1, device_id={"seq": lax.rem(my_seq + k, seqs)}, device_id_type=MESH
        )
    pl.semaphore_wait(barrier, reps + seqs - 2)

    def along_x(m, k):
        to = lax.rem(my_rep + k, reps)
        return pltpu.make_async_remote_copy(
            src_ref=grads_ref.at[m, to], dst_ref=got_x.at[m, k - 1],
            send_sem=x_send.at[m, k - 1], recv_sem=x_recv.at[m, k - 1],
            device_id={"rep": to}, device_id_type=MESH,
        )

    def along_z(m, k):
        to = lax.rem(my_seq + k, seqs)
        return pltpu.make_async_remote_copy(
            src_ref=part.at[m, to], dst_ref=got_z.at[m, k - 1],
            send_sem=z_send.at[m, k - 1], recv_sem=z_recv.at[m, k - 1],
            device_id={"seq": to}, device_id_type=MESH,
        )

    for m in range(2):
        for k in range(1, reps):
            along_x(m, k).start()
    for m in range(2):
        for k in range(1, reps):
            along_x(m, k).wait_recv()
        for p in range(seqs):
            total = grads_ref[m, my_rep, p].astype(F32)
            for k in range(1, reps):
                total = total + got_x[m, k - 1, p].astype(F32)
            part[m, p] = total.astype(BF16)
        for k in range(1, seqs):
            along_z(m, k).start()
    for m, ref in enumerate((in_ref, out_ref)):
        for k in range(1, seqs):
            along_z(m, k).wait_recv()
        total = part[m, my_seq].astype(F32)
        for k in range(1, seqs):
            total = total + got_z[m, k - 1].astype(F32)
        ref[...] = total
    for m in range(2):
        for k in range(1, reps):
            along_x(m, k).wait_send()
        for k in range(1, seqs):
            along_z(m, k).wait_send()


def local(
    query_rows, key_rows, value_rows, doc_lengths, residual, out_proj, router, expert_choice,
    weight_in, weight_out, grad_out,
):
    seqs, reps = lax.axis_size("seq"), lax.axis_size("rep")
    ranks = seqs * reps
    share = D // ranks
    experts = router.shape[1]
    chosen_col = expert_choice[0]
    chosen_row = chosen_col.reshape(1, T)
    grad_rows = grad_out[0]
    mixed, stats, send = pl.pallas_call(
        functools.partial(attend_body, ranks, reps, experts),
        out_shape=(
            jax.ShapeDtypeStruct((T, D), BF16),
            jax.ShapeDtypeStruct((T, 2 * T), F32),
            jax.ShapeDtypeStruct((experts * SLOTS, 2 * D), BF16),
        ),
        in_specs=[pl.BlockSpec(memory_space=pltpu.SMEM)] + [VMEM] * 9,
        out_specs=(VMEM,) * 3,
        scratch_shapes=[
            pltpu.VMEM((ranks, 3 * HD, T), BF16),
            pltpu.VMEM((ranks, 3 * HD, T), BF16),
            pltpu.VMEM((ranks, HD, T), BF16),
            pltpu.VMEM((ranks, HD, T), BF16),
            pltpu.VMEM((HD, ranks * T), BF16),
            pltpu.VMEM((ranks * T, HD), BF16),
            pltpu.VMEM((HD, ranks * T), BF16),
        ]
        + [pltpu.SemaphoreType.DMA((ranks,))] * 4,
        compiler_params=pltpu.CompilerParams(collective_id=1, has_side_effects=True),
        cost_estimate=pl.CostEstimate(
            flops=400000000, bytes_accessed=4000000, transcendentals=2000000
        ),
        name="attend",
    )(
        doc_lengths, query_rows[0], key_rows[0], value_rows[0], residual[0], out_proj, router,
        chosen_row, chosen_col, grad_rows,
    )
    got = lax.all_to_all(
        send.reshape(experts, SLOTS, 2 * D), "expert", split_axis=0, concat_axis=0, tiled=True
    )
    back, grads = pl.pallas_call(
        expert_body,
        out_shape=(
            jax.ShapeDtypeStruct((experts * SLOTS, 2 * D), BF16),
            jax.ShapeDtypeStruct((2, reps, seqs, share, FF), BF16),
        ),
        in_specs=[VMEM] * 3,
        out_specs=(VMEM,) * 2,
        scratch_shapes=[
            pltpu.VMEM((experts * SLOTS, FF), BF16),
            pltpu.VMEM((experts * SLOTS, FF), BF16),
        ],
        cost_estimate=pl.CostEstimate(flops=2400000000, bytes_accessed=5000000, transcendentals=400000),
        name="expert",
    )(got.reshape(experts * SLOTS, 2 * D), weight_in[0], weight_out[0])
    back = lax.all_to_all(
        back.reshape(experts, SLOTS, 2 * D), "expert", split_axis=0, concat_axis=0, tiled=True
    )
    share_in, share_out = pl.pallas_call(
        functools.partial(reduce_body, seqs, reps),
        out_shape=(jax.ShapeDtypeStruct((share, FF), F32),) * 2,
        in_specs=[VMEM],
        out_specs=(VMEM,) * 2,
        scratch_shapes=[
            pltpu.VMEM((2, reps - 1, seqs, share, FF), BF16),
            pltpu.VMEM((2, seqs, share, FF), BF16),
            pltpu.VMEM((2, seqs - 1, share, FF), BF16),
            pltpu.SemaphoreType.DMA((2, reps - 1)),
            pltpu.SemaphoreType.DMA((2, reps - 1)),
            pltpu.SemaphoreType.DMA((2, seqs - 1)),
            pltpu.SemaphoreType.DMA((2, seqs - 1)),
        ],
        compiler_params=pltpu.CompilerParams(collective_id=2, has_side_effects=True),
        cost_estimate=pl.CostEstimate(flops=20000000, bytes_accessed=40000000, transcendentals=0),
        name="grad_reduce",
    )(grads)
    layer_out, grad_mixed = pl.pallas_call(
        functools.partial(final_body, experts),
        out_shape=(jax.ShapeDtypeStruct((T, D), BF16),) * 2,
        in_specs=[VMEM] * 6,
        out_specs=(VMEM,) * 2,
        name="final",
    )(back.reshape(experts * SLOTS, 2 * D), mixed, stats, router, chosen_col, grad_rows)
    return (layer_out[None], grad_mixed[None], share_in[None], share_out[None])


def solution(mesh):
    rows = P("expert", ("seq", "rep"), None)
    weights = P("expert", None, None)
    in_specs = (
        rows, rows, rows, P("expert", None), rows, P(), P(), rows, weights, weights, rows,
    )
    return jax.shard_map(
        local, mesh=mesh, in_specs=in_specs, out_specs=(rows,) * 4, check_vma=False
    )
```

time: 226 us -> 160 us (0.71)
  Pallas kernels: 22.1 us -> 90.7 us
  waiting for transfers between devices: 60 us -> 1.09 us
  starting transfers between devices: 45.6 us -> 5.31 us
  blocking collectives: 87.5 us -> 55.5 us
    pallas_call x3 -> x2, Pallas kernels: 12.4 us -> 81 us  [the longest x1 42.9 us: local(): pl.pallas_call(functools.partial(attend_body, ranks, reps, experts), out_...]
    all_to_all x1, waiting for transfers between devices: 37.3 us -> 1.09 us  [local(): lax.all_to_all(back.reshape(experts, SLOTS, 2 * D), 'expert', split_axis=...]
    all_to_all x1 -> x0, blocking collectives: 32.7 us -> none  [local(): lax.all_to_all(grads.reshape(ranks, D // ranks, FF + D), group, split_axi...]
    all_to_all x2 -> x0, starting transfers between devices: 25.1 us -> none  [the longest x1 17.6 us: local(): lax.all_to_all(heads, group, split_axis=0, concat_axis=0, tiled=True)]
    all_to_all x2 -> x0, waiting for transfers between devices: 22.7 us -> none  [the longest x1 12.7 us: local(): lax.all_to_all(heads, group, split_axis=0, concat_axis=0, tiled=True)]
    all_to_all x1, starting transfers between devices: 20.6 us -> 5.31 us  [local(): lax.all_to_all(back.reshape(experts, SLOTS, 2 * D), 'expert', split_axis=...]
    transpose x3 -> x0, local copies, waits for them, and re-layouts: 3.08 us -> none  [the longest x1 1.03 us: local(): query_rows[0].T.reshape(H, HD, T)]
  transfers between devices with their start and end apart: 3 -> 1, of which waited for: 3 -> 1; matrix products, arithmetic and copies ran while one was open for 1% -> 0% of each run, Pallas kernels for 1% -> 24%
where the time goes in v2:
time: 160 us; the launch traced here: 159 us
  Pallas kernels  90.7 us (57%)
  blocking collectives  55.5 us (35%)
  local copies, waits for them, and re-layouts  5.36 us (3%)
  starting transfers between devices  5.31 us (3%)
    all_to_all x1, blocking collectives, local(): lax.all_to_all(send.reshape(experts, SLOTS, 2 * D), 'expert', split_axis=...  55.5 us
    pallas_call x1, Pallas kernels, local(): pl.pallas_call(functools.partial(attend_body, ranks, reps, experts), out_...  42.9 us
    pallas_call x1, Pallas kernels, local(): pl.pallas_call(functools.partial(reduce_body, seqs, reps), out_shape=(jax...  38.1 us
    pallas_call x1, Pallas kernels, local(): pl.pallas_call(expert_body, out_shape=(jax.ShapeDtypeStruct((experts * SL...  6.6 us
    all_to_all x1, starting transfers between devices, local(): lax.all_to_all(back.reshape(experts, SLOTS, 2 * D), 'expert', split_axis=...  5.31 us
    unnamed x9, local copies, waits for them, and re-layouts  3.97 us
  transfers between devices with their start and end apart: 1, of which 1 were waited for; matrix products, arithmetic and copies ran while one was open for 0% of the time, Pallas kernels for 24%

profile of v2, /device:TPU:1, one launch (start us, length us, event | category | flops | bytes accessed | tf_op | source)
XLA Modules:
  0.0 158.6 jit_solution(14623069192242747243)
XLA Ops:
  0.6 1.4 copy.16.col_ref
  2.0 1.5 copy.15.router_ref
  3.6 42.9 %attend.1 = (bf16[128,512]{1,0:T(8,128)(2,1)}, f32[128,256]{1,0:T(8,128)}, bf16[768,1024]{1,0:T(8,128)(2,1)}) custom-call(s32[1,8]{1,0:T(1,128)} %lengths_ref.1, bf16[128,512]{1,0:T(8,128)(2,1)} %bitcast.29, bf16[128,512]{1,0:T(8,128)(2,1)} %bitcast.30, bf16[128,512]{1,0:T(8,128)(2,1)} %bitcast.31, bf16[128,512]{1,0:T(8,128)(2,1)} %bitcast.32, ...), custom_call_target="tpu_custom_call" | custom-call | flops 400000000 | bytes 4000000 | tf_op jit(solution)/shard_map/attend/pallas_call | solution.py:345
  46.5 55.5 %all_to_all.10 = bf16[48,16,1024]{2,1,0:T(8,128)(2,1)} all-to-all(bf16[48,16,1024]{2,1,0:T(8,128)(2,1)} %bitcast.19), channel_id=1, replica_groups=mesh['seq'=4,'expert'=48,'rep'=4] {'expert'}, dimensions={0} | all-to-all | bytes 3145728 | tf_op jit(solution)/shard_map/all_to_all | solution.py:373
  102.0 6.6 %expert.1 = (bf16[768,1024]{1,0:T(8,128)(2,1)}, bf16[2,4,4,32,512]{4,3,2,1,0:T(8,128)(2,1)}) custom-call(bf16[768,1024]{1,0:T(8,128)(2,1)} %bitcast.20, bf16[512,512]{1,0:T(8,128)(2,1)} %bitcast.27, bf16[512,512]{1,0:T(8,128)(2,1)} %bitcast.28), custom_call_target="tpu_custom_call" | custom-call | flops 2400000000 | bytes 5000000 | tf_op jit(solution)/shard_map/expert/pallas_call | solution.py:376
  108.6 5.3 %all-to-all-start.1 = ((bf16[48,16,1024]{2,1,0:T(8,128)(2,1)}), bf16[48,16,1024]{2,1,0:T(8,128)(2,1)S(1)}, u32[]{:S(2)}, u32[]{:S(2)}) async-start(bf16[48,16,1024]{2,1,0:T(8,128)(2,1)} %bitcast.18), calls=%async_computation.1 | async-start | bytes 3145728 | tf_op jit(solution)/shard_map/all_to_all | solution.py:391
  113.9 38.1 %grad_reduce.1 = (f32[32,512]{1,0:T(8,128)}, f32[32,512]{1,0:T(8,128)}) custom-call(bf16[2,4,4,32,512]{4,3,2,1,0:T(8,128)(2,1)} %get-tuple-element.19.grads_ref), custom_call_target="tpu_custom_call" | custom-call | flops 20000000 | bytes 40000000 | tf_op jit(solution)/shard_map/grad_reduce/pallas_call | solution.py:394
  151.9 0.0 copy-start.2
  152.0 0.0 copy-start.1
  152.0 1.1 all-to-all-done.1
  153.1 0.0 copy-start
  153.1 1.1 copy-done
  154.2 3.1 %final.1 = (bf16[128,512]{1,0:T(8,128)(2,1)}, bf16[128,512]{1,0:T(8,128)(2,1)}) custom-call(bf16[768,1024]{1,0:T(8,128)(2,1)} %bitcast.17, bf16[128,512]{1,0:T(8,128)(2,1)} %get-tuple-element.15.mixed_ref, f32[128,256]{1,0:T(8,128)} %get-tuple-element.16.stats_ref, bf16[512,48]{1,0:T(8,128)(2,1)} %copy.15.router_ref, s32[128,1]{1,0:T(8,128)} %copy.16.col_ref, ...), custom_call_target="tpu_custom_call" | custom-call | tf_op jit(solution)/shard_map/final/pallas_call | solution.py:412
  157.3 0.0 copy-done.2
  157.3 0.6 copy.21
  157.9 0.0 copy-done.1
  158.0 0.6 copy.22
Async XLA Ops:
  108.6 44.5 %all-to-all-start.1 = ((bf16[48,16,1024]{2,1,0:T(8,128)(2,1)}), bf16[48,16,1024]{2,1,0:T(8,128)(2,1)S(1)}, u32[]{:S(2)}, u32[]{:S(2)}) async-start(bf16[48,16,1024]{2,1,0:T(8,128)(2,1)} %bitcast.18), calls=%async_computation.1 | async-start | bytes 3145728 | tf_op jit(solution)/shard_map/all_to_all | solution.py:391
  151.9 5.4 %copy-start.2 = (f32[32,512]{1,0:T(8,128)S(1)}, f32[32,512]{1,0:T(8,128)}, u32[]{:S(2)}) copy-start(f32[32,512]{1,0:T(8,128)} %get-tuple-element.20) | copy-start | bytes 196612
  152.0 6.0 %copy-start.1 = (f32[32,512]{1,0:T(8,128)S(1)}, f32[32,512]{1,0:T(8,128)}, u32[]{:S(2)}) copy-start(f32[32,512]{1,0:T(8,128)} %get-tuple-element.21) | copy-start | bytes 196612
  153.1 1.1 copy-start

commit v3 on v2

v3 whole, which is shorter than its diff:
```python
import functools
import math

import jax
import jax.numpy as jnp
from jax import lax
from jax.experimental import pallas as pl
from jax.experimental.pallas import tpu as pltpu
from jax.sharding import PartitionSpec as P

D = 512
H = 16
HD = 32
FF = 512
T = 128
EXPERTS = 48
CAP = 4
HOT = 16
PAIR = 2 * CAP
CORES = 2
DEPTH = 3
WINDOW = 1024
CHUNK = 256
MESH = pl.DeviceIdType.MESH
norm_eps = 1e-06
masked_score = -1e30
F32 = jnp.float32
BF16 = jnp.bfloat16
VMEM = pl.BlockSpec(memory_space=pltpu.VMEM)


def group_device(rank, reps):
    return {"seq": rank // reps, "rep": lax.rem(rank, reps)}


def attend_chunk(c, start, q_all, k_all, v_all):
    scale = math.log2(math.e) / math.sqrt(HD)
    first_q = c * CHUNK
    first_k = max(0, first_q - WINDOW)
    span = first_q + CHUNK - first_k
    queries = pl.ds(first_q, CHUNK)
    scores = jnp.dot(
        k_all[pl.ds(first_k, span), :], q_all[:, queries], preferred_element_type=F32
    )
    key_pos = lax.broadcasted_iota(jnp.int32, (span, CHUNK), 0) + first_k
    query_pos = lax.broadcasted_iota(jnp.int32, (span, CHUNK), 1) + first_q
    visible = (key_pos >= start) & (key_pos <= query_pos)
    scores = jnp.where(visible, scores, masked_score)
    top = jnp.max(scores, axis=0, keepdims=True)
    weights = jnp.exp2((scores - top) * scale)
    totals = jnp.sum(weights, axis=0, keepdims=True)
    result = jnp.dot(
        v_all[:, pl.ds(first_k, span)], weights.astype(BF16), preferred_element_type=F32
    )
    return (result / totals).astype(BF16)


def remote(src, dst, send_sem, recv_sem, device):
    return pltpu.make_async_remote_copy(
        src_ref=src, dst_ref=dst, send_sem=send_sem, recv_sem=recv_sem, device_id=device,
        device_id_type=MESH,
    )


def ones(mask):
    return mask.astype(F32).astype(BF16)


def step_body(
    seqs, reps, experts,
    lengths_ref, query_ref, key_ref, value_ref, residual_ref, proj_ref, router_ref, row_ref,
    grad_ref, up_hbm, down_hbm,
    out_ref, grad_mixed_ref, share_in_ref, share_out_ref,
    heads, got, result, att, q_all, k_all, v_all, up_ref, down_ref,
    cold_send, cold_got, made_send, made_got,
    hot_all, hot_res, core_got, y_send, y_got, z_send, z_got,
    act_ref, pre_ref, grads, got_x, part, got_zz,
    load_sem, send_sem, recv_sem, back_send_sem, back_recv_sem,
    cold_ssem, cold_rsem, made_ssem, made_rsem,
    hz_ssem, hz_rsem, ring_ssem, ring_rsem, hc_ssem, hc_rsem,
    core_ssem, core_rsem, y_ssem, y_rsem, z_ssem, z_rsem,
    x_ssem, x_rsem, zz_ssem, zz_rsem,
):
    blocks = seqs * reps
    my_seq = lax.axis_index("seq")
    my_rep = lax.axis_index("rep")
    me = my_seq * reps + my_rep
    mine = lax.axis_index("expert")
    row_size = CORES * DEPTH
    ys = experts // row_size
    my_y = mine // row_size
    my_z = lax.rem(mine, row_size) // CORES
    my_c = lax.rem(mine, CORES)

    def place_of(y, z, c):
        return {"expert": y * row_size + z * CORES + c}

    def hot_slot(c, y, z):
        return (c * ys + y) * DEPTH + z

    barrier = pltpu.get_barrier_semaphore()

    def greet(k, carry):
        pl.semaphore_signal(
            barrier, inc=1, device_id=group_device(lax.rem(me + k, blocks), reps),
            device_id_type=MESH,
        )
        return carry

    def greet_expert(k, carry):
        pl.semaphore_signal(
            barrier, inc=1, device_id={"expert": lax.rem(mine + k, experts)}, device_id_type=MESH
        )
        return carry

    lax.fori_loop(1, blocks, greet, 0)
    lax.fori_loop(1, experts, greet_expert, 0)
    load_up = pltpu.make_async_copy(up_hbm, up_ref, load_sem.at[0])
    load_down = pltpu.make_async_copy(down_hbm, down_ref, load_sem.at[1])
    load_up.start()
    load_down.start()
    for i, ref in enumerate((query_ref, key_ref, value_ref)):
        flipped = ref[...].astype(F32).T.astype(BF16)
        for h in range(blocks):
            heads[h, i * HD : (i + 1) * HD, :] = flipped[h * HD : (h + 1) * HD]
    starts = []
    for c in range(blocks * T // CHUNK):
        pos = lax.broadcasted_iota(jnp.int32, (1, CHUNK), 1) + c * CHUNK
        edge = jnp.int32(0)
        start = jnp.zeros((1, CHUNK), jnp.int32)
        for d in range(lengths_ref.shape[1] - 1):
            edge = edge + lengths_ref[0, d]
            start = jnp.where(pos >= edge, edge, start)
        starts.append(start)
    pl.semaphore_wait(barrier, blocks + experts - 2)

    def outgoing(k):
        to = lax.rem(me + k, blocks)
        return remote(
            heads.at[to], got.at[me], send_sem.at[to], recv_sem.at[me], group_device(to, reps)
        )

    def launch(k, carry):
        outgoing(k).start()
        return carry

    lax.fori_loop(1, blocks, launch, 0)
    got[me] = heads[me]

    def incoming(b):
        return remote(
            heads.at[b], got.at[b], send_sem.at[b], recv_sem.at[b], group_device(b, reps)
        )

    def returning(b):
        return remote(
            result.at[b], att.at[me], back_send_sem.at[b], back_recv_sem.at[me],
            group_device(b, reps),
        )

    per = CHUNK // T

    def give_back(c):
        for b in range(c * per, (c + 1) * per):

            @pl.when(me != b)
            def _():
                returning(b).start()

            @pl.when(me == b)
            def _():
                att[b] = result[b]

    chunks = blocks // per
    for c in range(chunks):
        for b in range(c * per, (c + 1) * per):

            @pl.when(me != b)
            def _():
                incoming(b).wait_recv()

            cols = pl.ds(b * T, T)
            q_all[:, cols] = got[b, 0:HD, :]
            v_all[:, cols] = got[b, 2 * HD : 3 * HD, :]
            k_all[cols, :] = got[b, HD : 2 * HD, :].astype(F32).T.astype(BF16)
        done = attend_chunk(c, starts[c], q_all, k_all, v_all)
        for j in range(per):
            result[c * per + j] = done[:, j * T : (j + 1) * T]
        if c:
            give_back(c - 1)

    chosen_row = row_ref[...]
    t_sub = lax.broadcasted_iota(jnp.int32, (T, T), 0)
    t_lane = lax.broadcasted_iota(jnp.int32, (T, T), 1)
    chosen_col = jnp.sum(jnp.where(t_sub == t_lane, chosen_row, 0), axis=1, keepdims=True)
    hits_t = chosen_row == lax.broadcasted_iota(jnp.int32, (experts, T), 0)
    hits = chosen_col == lax.broadcasted_iota(jnp.int32, (T, experts), 1)
    counts_t = jnp.sum(hits_t.astype(F32), axis=1, keepdims=True)
    counts = jnp.sum(hits.astype(F32), axis=0, keepdims=True)
    expert_ids = lax.broadcasted_iota(jnp.int32, (1, experts), 1)
    hot_id = jnp.max(jnp.where(counts > CAP, expert_ids, 0), axis=1, keepdims=True)
    hot_row = jnp.sum(jnp.where(hits_t, counts_t, 0.0), axis=0, keepdims=True) > CAP
    hot_col = jnp.sum(jnp.where(hits, counts, 0.0), axis=1, keepdims=True) > CAP
    ranks_t = jnp.dot(ones(hits_t), ones(t_sub < t_lane), preferred_element_type=F32)
    ranks = jnp.dot(ones(t_lane < t_sub), ones(hits), preferred_element_type=F32)
    rank_row = jnp.sum(jnp.where(hits_t, ranks_t, 0.0), axis=0, keepdims=True).astype(jnp.int32)
    rank_col = jnp.sum(jnp.where(hits, ranks, 0.0), axis=1, keepdims=True).astype(jnp.int32)
    nowhere = -1
    cold_slot_row = jnp.where(hot_row, nowhere, chosen_row * PAIR + rank_row)
    hot_slot_row = jnp.where(hot_row, rank_row, nowhere)
    cold_slot_col = jnp.where(hot_col, -PAIR, chosen_col * PAIR + rank_col)
    hot_slot_col = jnp.where(hot_col, rank_col, nowhere)
    slots = experts * PAIR
    slot_sub = lax.broadcasted_iota(jnp.int32, (slots, T), 0)
    place_rows = ones(slot_sub == cold_slot_row)
    place_grads = ones(
        slot_sub == jnp.where(hot_row, nowhere, chosen_row * PAIR + rank_row + CAP)
    )
    place_hot = ones(lax.broadcasted_iota(jnp.int32, (HOT, T), 0) == hot_slot_row)
    give_back(chunks - 1)

    def arrived(k, carry):
        b = lax.rem(me + k, blocks)
        remote(
            result.at[b], att.at[b], back_send_sem.at[b], back_recv_sem.at[b],
            group_device(b, reps),
        ).wait_recv()
        return carry

    lax.fori_loop(1, blocks, arrived, 0)
    attended = att[...].reshape(D, T).astype(F32).T.astype(BF16)
    mixed = (
        residual_ref[...].astype(F32)
        + jnp.dot(attended, proj_ref[...], preferred_element_type=F32)
    ).astype(BF16)
    mixed_f = mixed.astype(F32)
    inv_rms = lax.rsqrt(jnp.mean(mixed_f * mixed_f, axis=1, keepdims=True) + norm_eps)
    normed = (mixed_f * inv_rms).astype(BF16)
    last = (((1,), (1,)), ((), ()))
    first = (((0,), (0,)), ((), ()))
    logits = lax.dot_general(normed, router_ref[...], last, preferred_element_type=F32)
    gate = jax.nn.sigmoid(jnp.sum(jnp.where(hits, logits, 0.0), axis=1, keepdims=True))
    scaled = (gate * grad_ref[...].astype(F32)).astype(BF16)

    own_slot = hot_slot(my_c, my_y, my_z)
    hot_all[own_slot] = jnp.concatenate(
        [
            jnp.dot(place_hot, normed, preferred_element_type=F32),
            jnp.dot(place_hot, scaled, preferred_element_type=F32),
        ],
        axis=1,
    ).astype(BF16)
    placed = jnp.dot(place_rows, normed, preferred_element_type=F32) + jnp.dot(
        place_grads, scaled, preferred_element_type=F32
    )
    cold_send[...] = placed.astype(BF16).reshape(experts, PAIR, D)

    def z_copy(k):
        to = lax.rem(my_z + k, DEPTH)
        return remote(
            hot_all.at[own_slot], hot_all.at[own_slot], hz_ssem.at[k - 1], hz_rsem.at[my_z],
            place_of(my_y, to, my_c),
        )

    def z_arrival(z):
        slot = hot_slot(my_c, my_y, z)
        return remote(
            hot_all.at[slot], hot_all.at[slot], hz_ssem.at[0], hz_rsem.at[z],
            place_of(my_y, z, my_c),
        )

    def ring_copy(way, s, z):
        sign = 1 if way == 0 else -1
        block = lax.rem(my_y - sign * s + ys, ys)
        slot = hot_slot(my_c, block, z)
        return remote(
            hot_all.at[slot], hot_all.at[slot], ring_ssem.at[way, s, z], ring_rsem.at[way, s, z],
            place_of(lax.rem(my_y + sign + ys, ys), my_z, my_c),
        )

    def ring_block(way, s):
        sign = 1 if way == 0 else -1
        return lax.rem(my_y - sign * (s + 1) + ys, ys)

    def ring_arrival(way, s, z):
        sign = 1 if way == 0 else -1
        slot = hot_slot(my_c, ring_block(way, s), z)
        return remote(
            hot_all.at[slot], hot_all.at[slot], ring_ssem.at[way, s, z], ring_rsem.at[way, s, z],
            place_of(lax.rem(my_y - sign + ys, ys), my_z, my_c),
        )

    def to_sibling(y, z):
        slot = hot_slot(my_c, y, z)
        return remote(
            hot_all.at[slot], hot_all.at[slot], hc_ssem.at[y, z], hc_rsem.at[y, z],
            place_of(my_y, my_z, 1 - my_c),
        )

    def from_sibling(y, z):
        slot = hot_slot(1 - my_c, y, z)
        return remote(
            hot_all.at[slot], hot_all.at[slot], hc_ssem.at[y, z], hc_rsem.at[y, z],
            place_of(my_y, my_z, 1 - my_c),
        )

    for k in range(1, DEPTH):
        z_copy(k).start()

    def cold_copy(k):
        to = lax.rem(mine + k, experts)
        return remote(
            cold_send.at[to], cold_got.at[mine], cold_ssem.at[to], cold_rsem.at[mine],
            {"expert": to},
        )

    def start_cold(k, carry):
        cold_copy(k).start()
        return carry

    lax.fori_loop(1, experts, start_cold, 0)
    cold_got[mine] = cold_send[mine]
    ways = (ys // 2, ys - 1 - ys // 2)
    for t in range(DEPTH):
        z = lax.rem(my_z + t, DEPTH)
        if t:
            z_arrival(z).wait_recv()
        for way in range(2):
            ring_copy(way, 0, z).start()
        to_sibling(my_y, z).start()

    def ring_step(s):
        for t in range(DEPTH):
            z = lax.rem(my_z + t, DEPTH)
            for way in range(2):
                if s < ways[way]:
                    ring_arrival(way, s, z).wait_recv()
                    if s + 1 < ways[way]:
                        ring_copy(way, s + 1, z).start()
                    to_sibling(ring_block(way, s), z).start()

    for s in range(ways[0] - 1):
        ring_step(s)

    def cold_here(k, carry):
        b = lax.rem(mine + k, experts)
        remote(
            cold_send.at[b], cold_got.at[b], cold_ssem.at[b], cold_rsem.at[b], {"expert": b}
        ).wait_recv()
        return carry

    lax.fori_loop(1, experts, cold_here, 0)
    load_up.wait()
    load_down.wait()
    up = up_ref[...]
    down = down_ref[...]

    def expert_pass(tokens, grads_in):
        pre = jnp.dot(tokens, up, preferred_element_type=F32)
        sig = jax.nn.sigmoid(pre)
        activated = (pre * sig).astype(BF16)
        made = jnp.dot(activated, down, preferred_element_type=F32).astype(BF16)
        act_grad = lax.dot_general(grads_in, down, last, preferred_element_type=F32)
        pre_grad = (act_grad * sig * (1.0 + pre * (1.0 - sig))).astype(BF16)
        token_grad = lax.dot_general(pre_grad, up, last, preferred_element_type=F32).astype(BF16)
        return activated, pre_grad, made, token_grad

    cold_count = experts * CAP
    packed = cold_got[...].reshape(slots, D)
    cold_i = lax.broadcasted_iota(jnp.int32, (cold_count, slots), 0)
    pair_i = lax.broadcasted_iota(jnp.int32, (cold_count, slots), 1)
    spot = (cold_i // CAP) * PAIR + lax.rem(cold_i, CAP)
    take_rows = ones(pair_i == spot)
    take_grads = ones(pair_i == spot + CAP)
    cold_rows = jnp.dot(take_rows, packed, preferred_element_type=F32).astype(BF16)
    cold_grads = jnp.dot(take_grads, packed, preferred_element_type=F32).astype(BF16)
    cold_act, cold_pre, made, token_grad = expert_pass(cold_rows, cold_grads)
    repacked = lax.dot_general(take_rows, made, first, preferred_element_type=F32)
    repacked = repacked + lax.dot_general(
        take_grads, token_grad, first, preferred_element_type=F32
    )
    made_send[...] = repacked.astype(BF16).reshape(experts, PAIR, D)
    grad_up = lax.dot_general(cold_rows, cold_pre, first, preferred_element_type=F32)
    grad_down = lax.dot_general(cold_act, cold_grads, first, preferred_element_type=F32)

    def made_copy(k):
        to = lax.rem(mine + k, experts)
        return remote(
            made_send.at[to], made_got.at[mine], made_ssem.at[to], made_rsem.at[mine],
            {"expert": to},
        )

    def start_made(k, carry):
        made_copy(k).start()
        return carry

    lax.fori_loop(1, experts, start_made, 0)
    made_got[mine] = made_send[mine]
    ring_step(ways[0] - 1)
    for y in range(ys):
        for z in range(DEPTH):
            from_sibling(y, z).wait_recv()
    owner = (hot_id == mine).astype(F32)
    group = 16

    def hot_pass(i, carry):
        here = pl.ds(pl.multiple_of(i * group, group), group)
        flat = pl.ds(pl.multiple_of(i * group * HOT, group * HOT), group * HOT)
        both = hot_all[here].reshape(group * HOT, 2 * D)
        activated, pre_grad, hot_made, hot_grad = expert_pass(both[:, 0:D], both[:, D : 2 * D])
        hot_res[here, :, 0:D] = hot_made.reshape(group, HOT, D)
        hot_res[here, :, D : 2 * D] = hot_grad.reshape(group, HOT, D)
        act_ref[flat, :] = (activated.astype(F32) * owner).astype(BF16)
        pre_ref[flat, :] = (pre_grad.astype(F32) * owner).astype(BF16)
        return carry

    lax.fori_loop(0, experts // group, hot_pass, 0)
    hot_rows = hot_all[...].reshape(experts * HOT, 2 * D)
    grad_up = grad_up + lax.dot_general(
        hot_rows[:, 0:D], pre_ref[...], first, preferred_element_type=F32
    )

    half = experts // CORES
    core_copy = remote(
        hot_res.at[pl.ds((1 - my_c) * half, half)], core_got, core_ssem, core_rsem,
        place_of(my_y, my_z, 1 - my_c),
    )
    core_copy.start()
    grad_down = grad_down + lax.dot_general(
        act_ref[...], hot_rows[:, D : 2 * D], first, preferred_element_type=F32
    )
    share = D // blocks
    for m, grad in enumerate((grad_up, grad_down)):
        for j in range(blocks):
            grads[m, j % reps, j // reps] = grad[j * share : (j + 1) * share].astype(BF16)

    def along_x(m, k):
        to = lax.rem(my_rep + k, reps)
        return remote(
            grads.at[m, to], got_x.at[m, k - 1], x_ssem.at[m, k - 1], x_rsem.at[m, k - 1],
            {"rep": to},
        )

    def along_z(m, k):
        to = lax.rem(my_seq + k, seqs)
        return remote(
            part.at[m, to], got_zz.at[m, k - 1], zz_ssem.at[m, k - 1], zz_rsem.at[m, k - 1],
            {"seq": to},
        )

    hot_y = hot_id // row_size
    hot_z = lax.rem(hot_id, row_size) // CORES
    hot_c = lax.rem(hot_id, CORES)
    core_copy.wait_recv()
    for y in range(ys):
        for z in range(DEPTH):
            own = hot_res[hot_slot(my_c, y, z)].astype(F32)
            other = core_got[y * DEPTH + z].astype(F32)
            y_send[y, z] = jnp.where(hot_c == my_c, own, other).astype(BF16)
    for m in range(2):
        for k in range(1, reps):
            along_x(m, k).start()

    def y_copy(k):
        to = lax.rem(my_y + k, ys)
        return remote(
            y_send.at[to], y_got.at[my_y], y_ssem.at[to], y_rsem.at[my_y],
            place_of(to, my_z, my_c),
        )

    for k in range(1, ys):
        y_copy(k).start()
    y_got[my_y] = y_send[my_y]
    for m in range(2):
        for k in range(1, reps):
            along_x(m, k).wait_recv()
        for p in range(seqs):
            total = grads[m, my_rep, p].astype(F32)
            for k in range(1, reps):
                total = total + got_x[m, k - 1, p].astype(F32)
            part[m, p] = total.astype(BF16)
        for k in range(1, seqs):
            along_z(m, k).start()
    for k in range(1, ys):
        b = lax.rem(my_y + k, ys)
        remote(
            y_send.at[b], y_got.at[b], y_ssem.at[b], y_rsem.at[b], place_of(b, my_z, my_c)
        ).wait_recv()
    for z in range(DEPTH):
        kept = y_got[0, z].astype(F32)
        for y in range(1, ys):
            kept = jnp.where(hot_y == y, y_got[y, z].astype(F32), kept)
        z_send[z] = kept.astype(BF16)

    def made_here(k, carry):
        b = lax.rem(mine + k, experts)
        remote(
            made_send.at[b], made_got.at[b], made_ssem.at[b], made_rsem.at[b], {"expert": b}
        ).wait_recv()
        return carry

    lax.fori_loop(1, experts, made_here, 0)

    def down_copy(k):
        to = lax.rem(my_z + k, DEPTH)
        return remote(
            z_send.at[to], z_got.at[my_z], z_ssem.at[to], z_rsem.at[my_z],
            place_of(my_y, to, my_c),
        )

    for k in range(1, DEPTH):
        down_copy(k).start()
    z_got[my_z] = z_send[my_z]
    slot_lane = lax.broadcasted_iota(jnp.int32, (T, slots), 1)
    back = made_got[...].reshape(slots, D)
    result_f = jnp.dot(ones(slot_lane == cold_slot_col), back, preferred_element_type=F32)
    normed_grad = jnp.dot(
        ones(slot_lane == cold_slot_col + CAP), back, preferred_element_type=F32
    )
    router_cols = jnp.dot(ones(hits), router_ref[...], preferred_element_type=F32)
    for k in range(1, DEPTH):
        b = lax.rem(my_z + k, DEPTH)
        remote(
            z_send.at[b], z_got.at[b], z_ssem.at[b], z_rsem.at[b], place_of(my_y, b, my_c)
        ).wait_recv()
    kept = z_got[0].astype(F32)
    for z in range(1, DEPTH):
        kept = jnp.where(hot_z == z, z_got[z].astype(F32), kept)
    kept = kept.astype(BF16)
    pick_hot = ones(lax.broadcasted_iota(jnp.int32, (T, HOT), 1) == hot_slot_col)
    result_f = result_f + jnp.dot(pick_hot, kept[:, 0:D], preferred_element_type=F32)
    normed_grad = normed_grad + jnp.dot(
        pick_hot, kept[:, D : 2 * D], preferred_element_type=F32
    )
    grad_f = grad_ref[...].astype(F32)
    out_ref[...] = (mixed_f + gate * result_f).astype(BF16)
    gate_grad = jnp.sum(grad_f * result_f, axis=1, keepdims=True)
    logit_grad = gate_grad * gate * (1.0 - gate)
    total_grad = normed_grad + logit_grad * router_cols
    mean_term = jnp.mean(total_grad * mixed_f, axis=1, keepdims=True)
    input_grad = inv_rms * total_grad - mixed_f * inv_rms * inv_rms * inv_rms * mean_term
    grad_mixed_ref[...] = (grad_f + input_grad).astype(BF16)
    for m, ref in enumerate((share_in_ref, share_out_ref)):
        for k in range(1, seqs):
            along_z(m, k).wait_recv()
        total = part[m, my_seq].astype(F32)
        for k in range(1, seqs):
            total = total + got_zz[m, k - 1].astype(F32)
        ref[...] = total

    def sent_group(k, carry):
        outgoing(k).wait_send()
        returning(lax.rem(me + k, blocks)).wait_send()
        return carry

    def sent_experts(k, carry):
        cold_copy(k).wait_send()
        made_copy(k).wait_send()
        return carry

    lax.fori_loop(1, blocks, sent_group, 0)
    lax.fori_loop(1, experts, sent_experts, 0)
    for k in range(1, DEPTH):
        z_copy(k).wait_send()
        down_copy(k).wait_send()
    for way in range(2):
        for s in range(ways[way]):
            for z in range(DEPTH):
                ring_copy(way, s, z).wait_send()
    for y in range(ys):
        for z in range(DEPTH):
            to_sibling(y, z).wait_send()
    core_copy.wait_send()
    for k in range(1, ys):
        y_copy(k).wait_send()
    for m in range(2):
        for k in range(1, reps):
            along_x(m, k).wait_send()
        for k in range(1, seqs):
            along_z(m, k).wait_send()


def local(
    query_rows, key_rows, value_rows, doc_lengths, residual, out_proj, router, expert_choice,
    weight_in, weight_out, grad_out,
):
    seqs, reps = lax.axis_size("seq"), lax.axis_size("rep")
    blocks = seqs * reps
    experts = router.shape[1]
    share = D // blocks
    ys = experts // (CORES * DEPTH)
    dma = pltpu.SemaphoreType.DMA
    buffers = [
        (blocks, 3 * HD, T), (blocks, 3 * HD, T), (blocks, HD, T), (blocks, HD, T),
        (HD, blocks * T), (blocks * T, HD), (HD, blocks * T), (D, FF), (FF, D),
        (experts, PAIR, D), (experts, PAIR, D), (experts, PAIR, D), (experts, PAIR, D),
        (experts, HOT, 2 * D), (experts, HOT, 2 * D), (experts // CORES, HOT, 2 * D),
        (ys, DEPTH, HOT, 2 * D), (ys, DEPTH, HOT, 2 * D), (DEPTH, HOT, 2 * D),
        (DEPTH, HOT, 2 * D), (experts * HOT, FF), (experts * HOT, FF),
        (2, reps, seqs, share, FF), (2, reps - 1, seqs, share, FF), (2, seqs, share, FF),
        (2, seqs - 1, share, FF),
    ]
    semaphores = (
        [dma((2,))] + [dma((blocks,))] * 4 + [dma((experts,))] * 4
        + [dma((DEPTH - 1,)), dma((DEPTH,))]
        + [dma((2, ys // 2, DEPTH))] * 2 + [dma((ys, DEPTH))] * 2
        + [dma, dma] + [dma((ys,))] * 2 + [dma((DEPTH,))] * 2
        + [dma((2, reps - 1))] * 2 + [dma((2, seqs - 1))] * 2
    )
    anywhere = pl.BlockSpec(memory_space=pl.ANY)
    outs = pl.pallas_call(
        functools.partial(step_body, seqs, reps, experts),
        out_shape=(jax.ShapeDtypeStruct((T, D), BF16),) * 2
        + (jax.ShapeDtypeStruct((share, FF), F32),) * 2,
        in_specs=[pl.BlockSpec(memory_space=pltpu.SMEM)] + [VMEM] * 8 + [anywhere] * 2,
        out_specs=(VMEM,) * 4,
        scratch_shapes=[pltpu.VMEM(shape, BF16) for shape in buffers] + semaphores,
        compiler_params=pltpu.CompilerParams(collective_id=1, has_side_effects=True),
        name="step",
    )(
        doc_lengths, query_rows[0], key_rows[0], value_rows[0], residual[0], out_proj, router.T,
        expert_choice.reshape(1, T), grad_out[0], weight_in[0], weight_out[0],
    )
    return tuple(out[None] for out in outs)


def solution(mesh):
    rows = P("expert", ("seq", "rep"), None)
    weights = P("expert", None, None)
    in_specs = (
        rows, rows, rows, P("expert", None), rows, P(), P(), rows, weights, weights, rows,
    )
    return jax.shard_map(
        local, mesh=mesh, in_specs=in_specs, out_specs=(rows,) * 4, check_vma=False
    )
```

time: 160 us -> 115 us (0.72)
  blocking collectives: 55.5 us -> 0 us
  Pallas kernels: 90.7 us -> 110 us
  starting transfers between devices: 5.31 us -> 0 us
    all_to_all x1 -> x0, blocking collectives: 55.5 us -> none  [local(): lax.all_to_all(send.reshape(experts, SLOTS, 2 * D), 'expert', split_axis=...]
    pallas_call x4 -> x1, Pallas kernels: 90.7 us -> 110 us  [local(): pl.pallas_call(functools.partial(step_body, seqs, reps, experts), out_sha...]
    all_to_all x1 -> x0, starting transfers between devices: 5.31 us -> none  [local(): lax.all_to_all(back.reshape(experts, SLOTS, 2 * D), 'expert', split_axis=...]
    unnamed x9 -> x10, local copies, waits for them, and re-layouts: 3.97 us -> 3.96 us
  transfers between devices with their start and end apart: 1 -> 0, of which waited for: 1 -> 0; matrix products, arithmetic and copies ran while one was open for 0% -> 0% of each run, Pallas kernels for 24% -> 0%
where the time goes in v3:
time: 115 us; the launch traced here: 114 us
  Pallas kernels  110 us (96%)
  local copies, waits for them, and re-layouts  3.96 us (3%)
    pallas_call x1, Pallas kernels, local(): pl.pallas_call(functools.partial(step_body, seqs, reps, experts), out_sha...  110 us
    unnamed x10, local copies, waits for them, and re-layouts  3.96 us

profile of v3, /device:TPU:1, one launch (start us, length us, event | category | flops | bytes accessed | tf_op | source)
XLA Modules:
  0.0 114.5 jit_solution(274248017297699740)
XLA Ops:
  0.6 109.8 %step.1 = (bf16[128,512]{1,0:T(8,128)(2,1)}, bf16[128,512]{1,0:T(8,128)(2,1)}, f32[32,512]{1,0:T(8,128)}, f32[32,512]{1,0:T(8,128)}) custom-call(s32[1,8]{1,0:T(1,128)} %lengths_ref.1, bf16[128,512]{1,0:T(8,128)(2,1)} %bitcast.15, bf16[128,512]{1,0:T(8,128)(2,1)} %bitcast.16, bf16[128,512]{1,0:T(8,128)(2,1)} %bitcast.17, bf16[128,512]{1,0:T(8,128)(2,1)} %bitcast.18, ...), custom_call_target="tpu_custom_call" | custom-call | tf_op jit(solution)/shard_map/step/pallas_call | solution.py:611
  110.5 0.0 copy-start
  110.5 1.6 %copy.19 = bf16[1,128,512]{2,1,0:T(8,128)(2,1)} copy(bf16[1,128,512]{2,1,0:T(8,128)(2,1)} %bitcast.21) | data formatting | bytes 262144
  112.1 0.0 copy-done
  112.1 0.0 copy-start.2
  112.1 0.7 copy.20
  112.8 0.2 copy-done.2
  113.0 0.0 copy-start.1
  113.0 0.6 copy.21
  113.6 0.2 copy-done.1
  113.8 0.6 copy.22
Async XLA Ops:
  110.5 1.6 %copy-start = (bf16[128,512]{1,0:T(8,128)(2,1)S(1)}, bf16[128,512]{1,0:T(8,128)(2,1)}, u32[]{:S(2)}) copy-start(bf16[128,512]{1,0:T(8,128)(2,1)} %get-tuple-element.9) | copy-start | bytes 393220
  112.1 0.9 copy-start.2
  113.0 0.9 copy-start.1

commit v4 on v3

--- a/solution.py
+++ b/solution.py
@@ -304,30 +304,34 @@
             place_of(my_y, my_z, 1 - my_c),
         )
 
-    for k in range(1, DEPTH):
-        z_copy(k).start()
-
-    def cold_copy(k):
-        to = lax.rem(mine + k, experts)
-        return remote(
-            cold_send.at[to], cold_got.at[mine], cold_ssem.at[to], cold_rsem.at[mine],
-            {"expert": to},
-        )
-
-    def start_cold(k, carry):
-        cold_copy(k).start()
-        return carry
-
-    lax.fori_loop(1, experts, start_cold, 0)
-    cold_got[mine] = cold_send[mine]
-    ways = (ys // 2, ys - 1 - ys // 2)
-    for t in range(DEPTH):
+    def ring_start(t):
         z = lax.rem(my_z + t, DEPTH)
         if t:
             z_arrival(z).wait_recv()
         for way in range(2):
             ring_copy(way, 0, z).start()
         to_sibling(my_y, z).start()
+
+    for k in range(1, DEPTH):
+        z_copy(k).start()
+    ring_start(0)
+
+    def cold_copy(k):
+        to = lax.rem(mine + k, experts)
+        return remote(
+            cold_send.at[to], cold_got.at[mine], cold_ssem.at[to], cold_rsem.at[mine],
+            {"expert": to},
+        )
+
+    def start_cold(k, carry):
+        cold_copy(k).start()
+        return carry
+
+    lax.fori_loop(1, experts, start_cold, 0)
+    cold_got[mine] = cold_send[mine]
+    ways = (ys // 2, ys - 1 - ys // 2)
+    for t in range(1, DEPTH):
+        ring_start(t)
 
     def ring_step(s):
         for t in range(DEPTH):
@@ -339,9 +343,6 @@
                         ring_copy(way, s + 1, z).start()
                     to_sibling(ring_block(way, s), z).start()
 
-    for s in range(ways[0] - 1):
-        ring_step(s)
-
     def cold_here(k, carry):
         b = lax.rem(mine + k, experts)
         remote(
@@ -349,7 +350,6 @@
         ).wait_recv()
         return carry
 
-    lax.fori_loop(1, experts, cold_here, 0)
     load_up.wait()
     load_down.wait()
     up = up_ref[...]
@@ -365,6 +365,78 @@
         token_grad = lax.dot_general(pre_grad, up, last, preferred_element_type=F32).astype(BF16)
         return activated, pre_grad, made, token_grad
 
+    owner = (hot_id == mine).astype(F32)
+
+    def core_copy(b):
+        return remote(
+            hot_res.at[pl.ds(hot_slot(1 - my_c, b, 0), DEPTH)],
+            core_got.at[pl.ds(b * DEPTH, DEPTH)], core_ssem.at[b], core_rsem.at[b],
+            place_of(my_y, my_z, 1 - my_c),
+        )
+
+    def pair_of(p):
+        if p + 1 < ways[0]:
+            return [lax.rem(my_y - p - 1 + ys, ys), lax.rem(my_y + p + 1, ys)]
+        return [lax.rem(my_y + ways[0], ys), my_y]
+
+    def hot_pass(p):
+        where = []
+        for b in pair_of(p):
+            for z in range(DEPTH):
+                from_sibling(b, z).wait_recv()
+            where += [hot_slot(c, b, 0) for c in range(CORES)]
+        size = DEPTH * HOT
+        both = jnp.concatenate(
+            [hot_all[pl.ds(slot, DEPTH)].reshape(size, 2 * D) for slot in where], axis=0
+        )
+        activated, pre_grad, hot_made, hot_grad = expert_pass(both[:, 0:D], both[:, D : 2 * D])
+        kept_act = (activated.astype(F32) * owner).astype(BF16)
+        kept_pre = (pre_grad.astype(F32) * owner).astype(BF16)
+        for i, slot in enumerate(where):
+            rows = slice(i * size, (i + 1) * size)
+            here = pl.ds(slot, DEPTH)
+            hot_res[here, :, 0:D] = hot_made[rows].reshape(DEPTH, HOT, D)
+            hot_res[here, :, D : 2 * D] = hot_grad[rows].reshape(DEPTH, HOT, D)
+            act_ref[here] = kept_act[rows].reshape(DEPTH, HOT, FF)
+            pre_ref[here] = kept_pre[rows].reshape(DEPTH, HOT, FF)
+
+    def core_start(p):
+        for b in pair_of(p):
+            core_copy(b).start()
+
+    hot_y = hot_id // row_size
+    hot_z = lax.rem(hot_id, row_size) // CORES
+    hot_c = lax.rem(hot_id, CORES)
+
+    def y_copy(b):
+        return remote(
+            y_send.at[b], y_got.at[my_y], y_ssem.at[b], y_rsem.at[my_y],
+            place_of(b, my_z, my_c),
+        )
+
+    def y_fill(p):
+        for b in pair_of(p):
+            remote(
+                hot_res.at[pl.ds(hot_slot(1 - my_c, b, 0), DEPTH)],
+                core_got.at[pl.ds(b * DEPTH, DEPTH)], core_ssem.at[b], core_rsem.at[b],
+                place_of(my_y, my_z, 1 - my_c),
+            ).wait_recv()
+            own = hot_res[pl.ds(hot_slot(my_c, b, 0), DEPTH)].astype(F32)
+            other = core_got[pl.ds(b * DEPTH, DEPTH)].astype(F32)
+            y_send[b] = jnp.where(hot_c == my_c, own, other).astype(BF16)
+
+    def y_start(p):
+        here = pair_of(p)
+        if p + 1 == ways[0]:
+            here = here[:1]
+        for b in here:
+            y_copy(b).start()
+
+    ring_step(0)
+    ring_step(1)
+    hot_pass(0)
+    lax.fori_loop(1, experts, cold_here, 0)
+    core_start(0)
     cold_count = experts * CAP
     packed = cold_got[...].reshape(slots, D)
     cold_i = lax.broadcasted_iota(jnp.int32, (cold_count, slots), 0)
@@ -396,44 +468,30 @@
 
     lax.fori_loop(1, experts, start_made, 0)
     made_got[mine] = made_send[mine]
-    ring_step(ways[0] - 1)
-    for y in range(ys):
-        for z in range(DEPTH):
-            from_sibling(y, z).wait_recv()
-    owner = (hot_id == mine).astype(F32)
-    group = 16
-
-    def hot_pass(i, carry):
-        here = pl.ds(pl.multiple_of(i * group, group), group)
-        flat = pl.ds(pl.multiple_of(i * group * HOT, group * HOT), group * HOT)
-        both = hot_all[here].reshape(group * HOT, 2 * D)
-        activated, pre_grad, hot_made, hot_grad = expert_pass(both[:, 0:D], both[:, D : 2 * D])
-        hot_res[here, :, 0:D] = hot_made.reshape(group, HOT, D)
-        hot_res[here, :, D : 2 * D] = hot_grad.reshape(group, HOT, D)
-        act_ref[flat, :] = (activated.astype(F32) * owner).astype(BF16)
-        pre_ref[flat, :] = (pre_grad.astype(F32) * owner).astype(BF16)
-        return carry
-
-    lax.fori_loop(0, experts // group, hot_pass, 0)
-    hot_rows = hot_all[...].reshape(experts * HOT, 2 * D)
-    grad_up = grad_up + lax.dot_general(
-        hot_rows[:, 0:D], pre_ref[...], first, preferred_element_type=F32
-    )
-
-    half = experts // CORES
-    core_copy = remote(
-        hot_res.at[pl.ds((1 - my_c) * half, half)], core_got, core_ssem, core_rsem,
-        place_of(my_y, my_z, 1 - my_c),
-    )
-    core_copy.start()
-    grad_down = grad_down + lax.dot_general(
-        act_ref[...], hot_rows[:, D : 2 * D], first, preferred_element_type=F32
-    )
+    for p in range(1, ways[0] - 1):
+        ring_step(p + 1)
+        hot_pass(p)
+        y_fill(p - 1)
+        core_start(p)
+        y_start(p - 1)
+    hot_pass(ways[0] - 1)
+    y_fill(ways[0] - 2)
+    core_start(ways[0] - 1)
+    y_start(ways[0] - 2)
     share = D // blocks
-    for m, grad in enumerate((grad_up, grad_down)):
+
+    def store_grad(m, grad):
         for j in range(blocks):
             grads[m, j % reps, j // reps] = grad[j * share : (j + 1) * share].astype(BF16)
 
+    hot_count = experts * HOT
+    hot_rows = hot_all[...].reshape(hot_count, 2 * D)
+    grad_up = grad_up + lax.dot_general(
+        hot_rows[:, 0:D], pre_ref[...].reshape(hot_count, FF), first, preferred_element_type=F32
+    )
+    store_grad(0, grad_up)
+    y_fill(ways[0] - 1)
+
     def along_x(m, k):
         to = lax.rem(my_rep + k, reps)
         return remote(
@@ -448,29 +506,17 @@
             {"seq": to},
         )
 
-    hot_y = hot_id // row_size
-    hot_z = lax.rem(hot_id, row_size) // CORES
-    hot_c = lax.rem(hot_id, CORES)
-    core_copy.wait_recv()
-    for y in range(ys):
-        for z in range(DEPTH):
-            own = hot_res[hot_slot(my_c, y, z)].astype(F32)
-            other = core_got[y * DEPTH + z].astype(F32)
-            y_send[y, z] = jnp.where(hot_c == my_c, own, other).astype(BF16)
-    for m in range(2):
-        for k in range(1, reps):
-            along_x(m, k).start()
-
-    def y_copy(k):
-        to = lax.rem(my_y + k, ys)
-        return remote(
-            y_send.at[to], y_got.at[my_y], y_ssem.at[to], y_rsem.at[my_y],
-            place_of(to, my_z, my_c),
-        )
-
-    for k in range(1, ys):
-        y_copy(k).start()
+    for k in range(1, reps):
+        along_x(0, k).start()
+    y_start(ways[0] - 1)
+    grad_down = grad_down + lax.dot_general(
+        act_ref[...].reshape(hot_count, FF), hot_rows[:, D : 2 * D], first,
+        preferred_element_type=F32,
+    )
+    store_grad(1, grad_down)
     y_got[my_y] = y_send[my_y]
+    for k in range(1, reps):
+        along_x(1, k).start()
     for m in range(2):
         for k in range(1, reps):
             along_x(m, k).wait_recv()
@@ -570,9 +616,10 @@
     for y in range(ys):
         for z in range(DEPTH):
             to_sibling(y, z).wait_send()
-    core_copy.wait_send()
+    for b in range(ys):
+        core_copy(b).wait_send()
     for k in range(1, ys):
-        y_copy(k).wait_send()
+        y_copy(lax.rem(my_y + k, ys)).wait_send()
     for m in range(2):
         for k in range(1, reps):
             along_x(m, k).wait_send()
@@ -596,7 +643,7 @@
         (experts, PAIR, D), (experts, PAIR, D), (experts, PAIR, D), (experts, PAIR, D),
         (experts, HOT, 2 * D), (experts, HOT, 2 * D), (experts // CORES, HOT, 2 * D),
         (ys, DEPTH, HOT, 2 * D), (ys, DEPTH, HOT, 2 * D), (DEPTH, HOT, 2 * D),
-        (DEPTH, HOT, 2 * D), (experts * HOT, FF), (experts * HOT, FF),
+        (DEPTH, HOT, 2 * D), (experts, HOT, FF), (experts, HOT, FF),
         (2, reps, seqs, share, FF), (2, reps - 1, seqs, share, FF), (2, seqs, share, FF),
         (2, seqs - 1, share, FF),
     ]
@@ -604,7 +651,7 @@
         [dma((2,))] + [dma((blocks,))] * 4 + [dma((experts,))] * 4
         + [dma((DEPTH - 1,)), dma((DEPTH,))]
         + [dma((2, ys // 2, DEPTH))] * 2 + [dma((ys, DEPTH))] * 2
-        + [dma, dma] + [dma((ys,))] * 2 + [dma((DEPTH,))] * 2
+        + [dma((ys,))] * 4 + [dma((DEPTH,))] * 2
         + [dma((2, reps - 1))] * 2 + [dma((2, seqs - 1))] * 2
     )
     anywhere = pl.BlockSpec(memory_space=pl.ANY)

time: 115 us -> 116 us (level)
  no operation moved by 1% of the time
where the time goes in v4:
time: 116 us
  Pallas kernels  111 us (96%)
  local copies, waits for them, and re-layouts  3.96 us (3%)
    pallas_call x1, Pallas kernels, local(): pl.pallas_call(functools.partial(step_body, seqs, reps, experts), out_sha...  111 us
    unnamed x10, local copies, waits for them, and re-layouts  3.96 us

profile of v4, /device:TPU:1, one launch (start us, length us, event | category | flops | bytes accessed | tf_op | source)
XLA Modules:
  0.0 115.6 jit_solution(10908832932030878410)
XLA Ops:
  0.6 111.0 %step.1 = (bf16[128,512]{1,0:T(8,128)(2,1)}, bf16[128,512]{1,0:T(8,128)(2,1)}, f32[32,512]{1,0:T(8,128)}, f32[32,512]{1,0:T(8,128)}) custom-call(s32[1,8]{1,0:T(1,128)} %lengths_ref.1, bf16[128,512]{1,0:T(8,128)(2,1)} %bitcast.15, bf16[128,512]{1,0:T(8,128)(2,1)} %bitcast.16, bf16[128,512]{1,0:T(8,128)(2,1)} %bitcast.17, bf16[128,512]{1,0:T(8,128)(2,1)} %bitcast.18, ...), custom_call_target="tpu_custom_call" | custom-call | tf_op jit(solution)/shard_map/step/pallas_call | solution.py:658
  111.6 0.0 copy-start
  111.6 1.6 %copy.19 = bf16[1,128,512]{2,1,0:T(8,128)(2,1)} copy(bf16[1,128,512]{2,1,0:T(8,128)(2,1)} %bitcast.21) | data formatting | bytes 262144
  113.2 0.0 copy-done
  113.2 0.0 copy-start.2
  113.2 0.7 copy.20
  113.9 0.2 copy-done.2
  114.1 0.0 copy-start.1
  114.1 0.6 copy.21
  114.7 0.2 copy-done.1
  115.0 0.6 copy.22
Async XLA Ops:
  111.6 1.6 %copy-start = (bf16[128,512]{1,0:T(8,128)(2,1)S(1)}, bf16[128,512]{1,0:T(8,128)(2,1)}, u32[]{:S(2)}) copy-start(bf16[128,512]{1,0:T(8,128)(2,1)} %get-tuple-element.9) | copy-start | bytes 393220
  113.2 0.9 copy-start.2
  114.1 0.9 copy-start.1

commit v5 on v4

--- a/solution.py
+++ b/solution.py
@@ -435,8 +435,9 @@
     ring_step(0)
     ring_step(1)
     hot_pass(0)
+    core_start(0)
+    ring_step(2)
     lax.fori_loop(1, experts, cold_here, 0)
-    core_start(0)
     cold_count = experts * CAP
     packed = cold_got[...].reshape(slots, D)
     cold_i = lax.broadcasted_iota(jnp.int32, (cold_count, slots), 0)
@@ -469,7 +470,8 @@
     lax.fori_loop(1, experts, start_made, 0)
     made_got[mine] = made_send[mine]
     for p in range(1, ways[0] - 1):
-        ring_step(p + 1)
+        if p > 1:
+            ring_step(p + 1)
         hot_pass(p)
         y_fill(p - 1)
         core_start(p)
@@ -490,7 +492,6 @@
         hot_rows[:, 0:D], pre_ref[...].reshape(hot_count, FF), first, preferred_element_type=F32
     )
     store_grad(0, grad_up)
-    y_fill(ways[0] - 1)
 
     def along_x(m, k):
         to = lax.rem(my_rep + k, reps)
@@ -508,11 +509,12 @@
 
     for k in range(1, reps):
         along_x(0, k).start()
-    y_start(ways[0] - 1)
+    y_fill(ways[0] - 1)
     grad_down = grad_down + lax.dot_general(
         act_ref[...].reshape(hot_count, FF), hot_rows[:, D : 2 * D], first,
         preferred_element_type=F32,
     )
+    y_start(ways[0] - 1)
     store_grad(1, grad_down)
     y_got[my_y] = y_send[my_y]
     for k in range(1, reps):

time: 116 us -> 115 us (level)
  no operation moved by 1% of the time
where the time goes in v5:
time: 115 us
  Pallas kernels  110 us (96%)
  local copies, waits for them, and re-layouts  3.96 us (3%)
    pallas_call x1, Pallas kernels, local(): pl.pallas_call(functools.partial(step_body, seqs, reps, experts), out_sha...  110 us
    unnamed x10, local copies, waits for them, and re-layouts  3.96 us

profile of v5, /device:TPU:1, one launch (start us, length us, event | category | flops | bytes accessed | tf_op | source)
XLA Modules:
  0.0 114.9 jit_solution(1276072428051036320)
XLA Ops:
  0.6 110.3 %step.1 = (bf16[128,512]{1,0:T(8,128)(2,1)}, bf16[128,512]{1,0:T(8,128)(2,1)}, f32[32,512]{1,0:T(8,128)}, f32[32,512]{1,0:T(8,128)}) custom-call(s32[1,8]{1,0:T(1,128)} %lengths_ref.1, bf16[128,512]{1,0:T(8,128)(2,1)} %bitcast.15, bf16[128,512]{1,0:T(8,128)(2,1)} %bitcast.16, bf16[128,512]{1,0:T(8,128)(2,1)} %bitcast.17, bf16[128,512]{1,0:T(8,128)(2,1)} %bitcast.18, ...), custom_call_target="tpu_custom_call" | custom-call | tf_op jit(solution)/shard_map/step/pallas_call | solution.py:660
  110.9 0.0 copy-start
  110.9 1.6 %copy.19 = bf16[1,128,512]{2,1,0:T(8,128)(2,1)} copy(bf16[1,128,512]{2,1,0:T(8,128)(2,1)} %bitcast.21) | data formatting | bytes 262144
  112.5 0.0 copy-done
  112.6 0.0 copy-start.2
  112.6 0.7 copy.20
  113.2 0.2 copy-done.2
  113.4 0.0 copy-start.1
  113.4 0.6 copy.21
  114.0 0.2 copy-done.1
  114.3 0.6 copy.22
Async XLA Ops:
  110.9 1.6 %copy-start = (bf16[128,512]{1,0:T(8,128)(2,1)S(1)}, bf16[128,512]{1,0:T(8,128)(2,1)}, u32[]{:S(2)}) copy-start(bf16[128,512]{1,0:T(8,128)(2,1)} %get-tuple-element.9) | copy-start | bytes 393220
  112.6 0.9 copy-start.2
  113.4 0.9 copy-start.1
